TPU v7x, 32 devices: a whole 2x2x4 slice. The times are simulated.
32 devices in a mesh: ctx: 16 (over z, y, core), wa: 2 (over x).
Axes of the slice: x: 2, y: 2, z: 4, core: 2. Of those that a mesh axis runs over, the one named last changes fastest.
Arguments:
- query_in: bfloat16 [2, 4096, 512], P('wa', 'ctx'), may hold values from -6 to 6
- content_in: bfloat16 [2, 4096, 512], P('wa', 'ctx'), may hold values from -6 to 6
- encoder_in: bfloat16 [2, 4096, 512], P('wa', 'ctx'), may hold values from -6 to 6
- out_grad: bfloat16 [2, 4096, 512], P('wa', 'ctx'), may hold values from -6 to 6
- document_lengths: int32 [2, 4], P('wa'), may hold values from 1 to 2048, 4096 in all within a row
- key_ranks: int32 [2, 4096], P('wa'), may hold values from 0 to 15
- query_limits: int32 [2, 4096], P('wa'), may hold values from 1 to 16
- self_query_weight: bfloat16 [512, 512], P('wa'), may hold values from -0.25 to 0.25
- self_query_bias: bfloat16 [512], P('wa'), may hold values from -3 to 3
- self_key_weight: bfloat16 [512, 512], P('wa'), may hold values from -0.25 to 0.25
- self_value_weight: bfloat16 [512, 512], P('wa'), may hold values from -0.25 to 0.25
- self_value_bias: bfloat16 [512], P('wa'), may hold values from -0.29882812 to 0.29882812
- self_out_weight: bfloat16 [512, 512], P('wa'), may hold values from -3 to 3
- self_out_bias: bfloat16 [512], P('wa'), may hold values from -3 to 3
- norm_one_gain: bfloat16 [512], P('wa'), may hold values from 0.099609375 to 1.8984375
- norm_one_shift: bfloat16 [512], P('wa'), may hold values from -2 to 2
- cross_query_weight: bfloat16 [512, 512], P('wa'), may hold values from -0.25 to 0.25
- cross_query_bias: bfloat16 [512], P('wa'), may hold values from -3 to 3
- cross_key_weight: bfloat16 [512, 512], P('wa'), may hold values from -0.25 to 0.25
- cross_value_weight: bfloat16 [512, 512], P('wa'), may hold values from -0.25 to 0.25
- cross_value_bias: bfloat16 [512], P('wa'), may hold values from -0.29882812 to 0.29882812
- cross_out_weight: bfloat16 [512, 512], P('wa'), may hold values from -3 to 3
- cross_out_bias: bfloat16 [512], P('wa'), may hold values from -3 to 3
- norm_two_gain: bfloat16 [512], P('wa'), may hold values from 0.099609375 to 1.8984375
- norm_two_shift: bfloat16 [512], P('wa'), may hold values from -2 to 2
- expand_weight: bfloat16 [512, 2048], P('wa'), may hold values from -0.25 to 0.25
- expand_bias: bfloat16 [2048], P('wa'), may hold values from -2 to 2
- shrink_weight: bfloat16 [2048, 512], P('wa'), may hold values from -0.125 to 0.125
- shrink_bias: bfloat16 [512], P('wa'), may hold values from -2 to 2
- norm_three_gain: bfloat16 [512], P('wa'), may hold values from 0.099609375 to 1.8984375
- norm_three_shift: bfloat16 [512], P('wa'), may hold values from -2 to 2
Outputs:
- layer_out: float32 [2, 4096, 512], P('wa', 'ctx')
- query_grad: float32 [2, 4096, 512], P('wa', 'ctx')
- content_grad: float32 [2, 4096, 512], P('wa', 'ctx')
- encoder_grad: float32 [2, 4096, 512], P('wa', 'ctx')
- grad_self_query_weight: float32 [512, 512], P('wa')
- grad_self_query_bias: float32 [512], P('wa')
- grad_self_key_weight: float32 [512, 512], P('wa')
- grad_self_value_weight: float32 [512, 512], P('wa')
- grad_self_value_bias: float32 [512], P('wa')
- grad_self_out_weight: float32 [512, 512], P('wa')
- grad_self_out_bias: float32 [512], P('wa')
- grad_norm_one_gain: float32 [512], P('wa')
- grad_norm_one_shift: float32 [512], P('wa')
- grad_cross_query_weight: float32 [512, 512], P('wa')
- grad_cross_query_bias: float32 [512], P('wa')
- grad_cross_key_weight: float32 [512, 512], P('wa')
- grad_cross_value_weight: float32 [512, 512], P('wa')
- grad_cross_value_bias: float32 [512], P('wa')
- grad_cross_out_weight: float32 [512, 512], P('wa')
- grad_cross_out_bias: float32 [512], P('wa')
- grad_norm_two_gain: float32 [512], P('wa')
- grad_norm_two_shift: float32 [512], P('wa')
- grad_expand_weight: float32 [512, 2048], P('wa')
- grad_expand_bias: float32 [2048], P('wa')
- grad_shrink_weight: float32 [2048, 512], P('wa')
- grad_shrink_bias: float32 [512], P('wa')
- grad_norm_three_gain: float32 [512], P('wa')
- grad_norm_three_shift: float32 [512], P('wa')
Inputs may be any that keep to these rules, and one draw needn't show every extreme that they name: `document_lengths`: each row gives the 4 document lengths of one packed sequence in order; they sum to 4096, and the longest is exactly 2048.
All inputs are finite; a program needn't handle non-finite values.
Results may differ from a plain program's by a relative error of at most 0.03.
Values may be sent and summed in bfloat16 or wider, within the bound.
A program may use at most 320 MiB of HBM per device.

v0:
```python
import functools
import jax
import jax.numpy as jnp
from jax import lax
from jax.experimental import pallas as pl
from jax.experimental.pallas import tpu as pltpu
from jax.sharding import Mesh
from jax.sharding import PartitionSpec as P

PLANE = 4
DOCLEN = 2048
EPSILON = 1e-05
ROOT_HALF = 0.7071067811865476
INV_ROOT_TWO_PI = 0.3989422804014327
NEGATIVE = -1e29
HIDE = -(2.0 ** 100)
BLOCK = 256
WIDE = 512
STAT = 40


def dot(a, b, ca, cb):
    return lax.dot_general(a, b, (((ca,), (cb,)), ((), ())), preferred_element_type=jnp.float32)


def left_half(shape):
    return lax.broadcasted_iota(jnp.int32, shape, 1) < 64


def spans(lens_ref, first, count):
    low, high, total = 0, 0, 0
    for d in range(lens_ref.shape[1]):
        begin = total
        total = total + lens_ref[0, d]
        low = jnp.where(begin <= first, begin, low)
        high = jnp.where(begin <= first + count - 1, total, high)
    return low, high


def openings(lens_ref, places):
    total, found = 0, places == 0
    for d in range(lens_ref.shape[1] - 1):
        total = total + lens_ref[0, d]
        found = jnp.logical_or(found, places == total)
    return found


def over_blocks(low, high, first, size, step, carry, ranked):
    begin, end = low // size, (high + size - 1) // size
    own = first // size
    skip = 1 if ranked else 0

    def body(index, carry):
        if ranked:
            index = index + jnp.where(index >= own, 1, 0)
        return step(pl.multiple_of(index * size, size), carry)

    carry = lax.fori_loop(begin, end - skip, body, carry)
    if ranked:
        carry = step(pl.multiple_of(own * size, size), carry, True)
    return carry


def forward_kernel(ranked, lens_ref, own_ref, q_ref, qm_ref, kv_ref, km_ref, o_ref, lse_ref):
    rows = q_ref.shape[0]
    base = own_ref[0] * rows
    half = left_half((BLOCK, 128))
    khalf = left_half((WIDE, 128))
    one = jnp.ones((WIDE, 128), jnp.bfloat16)

    def one_block(block, _):
        start = pl.multiple_of(block * BLOCK, BLOCK)
        first = base + start
        low, high = spans(lens_ref, first, BLOCK)
        q = q_ref[pl.ds(start, BLOCK), :]
        qm = qm_ref[pl.ds(start, BLOCK), :]
        queries = (jnp.where(half, q, qm), jnp.where(half, qm, q))

        def step(at, carry, diagonal=False):
            k = kv_ref[pl.ds(at, WIDE), :128]
            v = kv_ref[pl.ds(at, WIDE), 128:]
            km = km_ref[pl.ds(at, WIDE), :]
            keys = (jnp.where(khalf, k, km), jnp.where(khalf, km, k))
            values = (jnp.where(khalf, v, one), jnp.where(khalf, one, v))
            scores = [dot(queries[h], keys[h], 1, 1) for h in (0, 1)]
            if diagonal:
                place = first + lax.broadcasted_iota(jnp.int32, (BLOCK, WIDE), 0)
                other = at + lax.broadcasted_iota(jnp.int32, (BLOCK, WIDE), 1)
                column = first + lax.broadcasted_iota(jnp.int32, (BLOCK, 1), 0)
                banned = jnp.where(openings(lens_ref, column), -1, place) == other
                scores = [jnp.where(banned, HIDE, s) for s in scores]
            out = []
            for h in (0, 1):
                peak, acc = carry[h]
                new = jnp.maximum(peak, jnp.max(scores[h], axis=1, keepdims=True))
                p = jnp.exp(scores[h] - new).astype(jnp.bfloat16)
                acc = acc * jnp.exp(peak - new) + dot(p, values[h], 1, 0)
                out.append((new, acc))
            return tuple(out)

        empty = (jnp.full((BLOCK, 1), NEGATIVE, jnp.float32), jnp.zeros((BLOCK, 128), jnp.float32))
        (peak0, acc0), (peak1, acc1) = over_blocks(low, high, first, WIDE, step, (empty, empty), ranked)
        total = jnp.where(half, acc1, acc0)
        mixed = jnp.where(half, acc0, acc1)
        o_ref[pl.ds(start, BLOCK), :] = mixed / pltpu.roll(total, 64, 1)
        lse_ref[pl.ds(start, BLOCK), :] = jnp.where(half, peak1, peak0) + jnp.log(total)
        return 0

    lax.fori_loop(0, rows // BLOCK, one_block, 0)


def attend_forward(ranked, lens, own, q, qm, kv, km):
    rows = q.shape[0]
    whole = pl.BlockSpec(memory_space=pltpu.VMEM)
    smem = pl.BlockSpec(memory_space=pltpu.SMEM)
    return pl.pallas_call(
        functools.partial(forward_kernel, ranked),
        out_shape=(jax.ShapeDtypeStruct((rows, 128), jnp.float32),) * 2,
        in_specs=[smem, smem] + [whole] * 4,
        out_specs=(whole, whole),
        cost_estimate=pl.CostEstimate(flops=12000000000, bytes_accessed=0, transcendentals=0),
        compiler_params=pltpu.CompilerParams(vmem_limit_bytes=60 << 20),
    )(lens, own, q, qm, kv, km)


def with_stat(marks, stat, lane, at):
    high = stat.astype(jnp.bfloat16)
    rest = stat - high.astype(jnp.float32)
    middle = rest.astype(jnp.bfloat16)
    tail = (rest - middle.astype(jnp.float32)).astype(jnp.bfloat16)
    side = jnp.where(lane == at, high, jnp.where(lane == at + 1, middle, jnp.where(lane == at + 2, tail, marks)))
    return side


def backward_kernel(ranked, lens_ref, own_ref, q_ref, qm_ref, kv_ref, km_ref, o_ref, lse_ref, do_ref,
                    dq_ref, dkv_ref, own_dkv_ref, dk_ref, dv_ref):
    rows = q_ref.shape[0]
    base = own_ref[0] * rows
    half = left_half((BLOCK, 128))
    lane = lax.broadcasted_iota(jnp.int32, (BLOCK, 128), 1)
    one = jnp.ones((BLOCK, 128), jnp.bfloat16)
    zero = jnp.zeros((BLOCK, 128), jnp.bfloat16)

    def clear(index, _):
        at = pl.multiple_of(index * BLOCK, BLOCK)
        dk_ref[pl.ds(at, BLOCK), :] = jnp.zeros((BLOCK, 128), jnp.float32)
        dv_ref[pl.ds(at, BLOCK), :] = jnp.zeros((BLOCK, 128), jnp.float32)
        return 0

    lax.fori_loop(0, kv_ref.shape[0] // BLOCK, clear, 0)

    def one_block(block, _):
        start = pl.multiple_of(block * BLOCK, BLOCK)
        first = base + start
        low, high = spans(lens_ref, first, BLOCK)
        here = pl.ds(start, BLOCK)
        q, qm, do, lse = q_ref[here, :], qm_ref[here, :], do_ref[here, :], lse_ref[here, :]
        shared = do.astype(jnp.float32) * o_ref[here, :]
        delta0 = jnp.sum(jnp.where(half, shared, 0.0), axis=1, keepdims=True)
        delta1 = jnp.sum(jnp.where(half, 0.0, shared), axis=1, keepdims=True)
        side = with_stat(qm, lse, lane % 64, STAT)
        queries = (jnp.where(half, q, side), jnp.where(half, side, q))
        side = with_stat(zero, -jnp.where(half, delta1, delta0), lane % 64, STAT)
        grads = (jnp.where(half, do, side), jnp.where(half, side, do))

        def step(at, carry, diagonal=False):
            there = pl.ds(at, BLOCK)
            k, v, km = kv_ref[there, :128], kv_ref[there, 128:], km_ref[there, :]
            keys = (jnp.where(half, k, km), jnp.where(half, km, k))
            values = (jnp.where(half, v, one), jnp.where(half, one, v))
            scores = [dot(keys[h], queries[h], 1, 1) for h in (0, 1)]
            if diagonal:
                other = first + lax.broadcasted_iota(jnp.int32, (BLOCK, BLOCK), 0)
                row = first + lax.broadcasted_iota(jnp.int32, (1, BLOCK), 1)
                banned = other == jnp.where(openings(lens_ref, row), -1, row)
                scores = [jnp.where(banned, HIDE, s) for s in scores]
            dvs, dks, dqs = [], [], []
            for h in (0, 1):
                p = jnp.exp(scores[h])
                dp = dot(values[h], grads[h], 1, 1)
                ds = (p * dp).astype(jnp.bfloat16)
                dvs.append(dot(p.astype(jnp.bfloat16), do, 1, 0))
                dks.append(dot(ds, q, 1, 0))
                dqs.append(dot(ds, k, 0, 0))
            dv_ref[there, :] += jnp.where(half, dvs[0], dvs[1])
            dk_ref[there, :] += jnp.where(half, dks[0], dks[1])
            return carry + jnp.where(half, dqs[0], dqs[1])

        dq = over_blocks(low, high, first, BLOCK, step, jnp.zeros((BLOCK, 128), jnp.float32), ranked)
        dq_ref[here, :] = (dq * 0.125).astype(dq_ref.dtype)
        return 0

    lax.fori_loop(0, rows // BLOCK, one_block, 0)

    def save(index, _):
        there = pl.ds(pl.multiple_of(index * BLOCK, BLOCK), BLOCK)
        dkv_ref[there, :128] = dk_ref[there, :].astype(jnp.bfloat16)
        dkv_ref[there, 128:] = dv_ref[there, :].astype(jnp.bfloat16)
        return 0

    lax.fori_loop(0, kv_ref.shape[0] // BLOCK, save, 0)
    mine = pl.ds(pl.multiple_of(base, BLOCK), rows)
    own_dkv_ref[:, :128] = dk_ref[mine, :]
    own_dkv_ref[:, 128:] = dv_ref[mine, :]


def attend_backward(ranked, lens, own, q, qm, kv, km, o, lse, do):
    rows, keys = q.shape[0], kv.shape[0]
    whole = pl.BlockSpec(memory_space=pltpu.VMEM)
    smem = pl.BlockSpec(memory_space=pltpu.SMEM)
    return pl.pallas_call(
        functools.partial(backward_kernel, ranked),
        out_shape=(jax.ShapeDtypeStruct((rows, 128), jnp.bfloat16),) + (
            jax.ShapeDtypeStruct((keys, 256), jnp.bfloat16), jax.ShapeDtypeStruct((rows, 256), jnp.float32)),
        in_specs=[smem, smem] + [whole] * 7,
        out_specs=(whole, whole, whole),
        scratch_shapes=[pltpu.VMEM((keys, 128), jnp.float32)] * 2,
        cost_estimate=pl.CostEstimate(flops=26000000000, bytes_accessed=0, transcendentals=0),
        compiler_params=pltpu.CompilerParams(vmem_limit_bytes=60 << 20),
    )(lens, own, q, qm, kv, km, o, lse, do)


def matmul(left, right):
    return jnp.dot(left, right, preferred_element_type=jnp.float32)


def left_product(left, right):
    return jnp.einsum("ta,tb->ab", left, right, preferred_element_type=jnp.float32)


def right_product(left, right):
    return jnp.einsum("ta,ba->tb", left, right, preferred_element_type=jnp.float32)


def column_sum(value):
    return jnp.sum(value.astype(jnp.float32), axis=0)


def gelu_slope(value):
    cumulative = 0.5 * (1.0 + lax.erf(value * ROOT_HALF))
    return cumulative + value * jnp.exp(-0.5 * value * value) * INV_ROOT_TWO_PI


def norm_forward(value, gain_row, shift_row):
    middle = jnp.mean(value, axis=-1, keepdims=True)
    centred = value - middle
    spread = jnp.mean(centred * centred, axis=-1, keepdims=True)
    inverse = lax.rsqrt(spread + EPSILON)
    normed = centred * inverse
    return (normed * gain_row + shift_row, normed, inverse)


def norm_backward(incoming, normed, inverse, gain_row):
    scaled = incoming * gain_row
    centred = (
        scaled
        - jnp.mean(scaled, axis=-1, keepdims=True)
        - normed * jnp.mean(scaled * normed, axis=-1, keepdims=True)
    )
    return (inverse * centred, jnp.sum(incoming * normed, axis=0), jnp.sum(incoming, axis=0))


MESH = pl.DeviceIdType.MESH
ANY = pl.BlockSpec(memory_space=pltpu.HBM)
VMEM = pl.BlockSpec(memory_space=pltpu.VMEM)
SMEM = pl.BlockSpec(memory_space=pltpu.SMEM)
DMA = pltpu.SemaphoreType.DMA


def across(place, offset):
    if offset == 1:
        return place + 1 - 2 * lax.rem(place, 2)
    if offset == 2:
        return lax.rem(place + 2, 4)
    return 3 - place


def remote(src, dst, sends, recvs, where):
    return pltpu.make_async_remote_copy(
        src_ref=src, dst_ref=dst, send_sem=sends, recv_sem=recvs, device_id=where, device_id_type=MESH)


def greet(grp_count, wa_count, plane=True, groups=True, rows=True):
    barrier = pltpu.get_barrier_semaphore()
    grp, pln, wa = lax.axis_index("grp"), lax.axis_index("pln"), lax.axis_index("wa")

    def hello(where):
        pl.semaphore_signal(barrier, inc=1, device_id=where, device_id_type=MESH)

    count = 0
    if plane:
        for offset in (1, 2, 3):
            hello({"pln": across(pln, offset)})
        count += 3
    if rows:
        for offset in range(1, wa_count):
            hello({"wa": lax.rem(wa + offset, wa_count)})
        count += wa_count - 1
    if groups:
        @pl.when(grp > 0)
        def _():
            hello({"grp": grp - 1})

        @pl.when(grp < grp_count - 1)
        def _():
            hello({"grp": grp + 1})

        count = count + jnp.where(grp > 0, 1, 0) + jnp.where(grp < grp_count - 1, 1, 0)
    pl.semaphore_wait(barrier, count)


class Rows:
    def __init__(self, shard, full, sems, index, wa_count, stage=None):
        self.shard, self.full, self.sems, self.index, self.wa_count = shard, full, sems, index, wa_count
        self.stage = stage
        self.size = shard.shape[0]
        self.half = self.size // 2
        self.wa, self.pln = lax.axis_index("wa"), lax.axis_index("pln")
        self.core = lax.rem(self.pln, 2)

    def part(self, owner, core):
        return pl.ds(pl.multiple_of(owner * self.size + core * self.half, 16), self.half)

    def keep(self):
        own = pl.ds(pl.multiple_of(self.wa * self.size, 16), self.size)
        source = self.shard if self.stage is None else self.stage
        return pltpu.make_async_copy(source, self.full.at[own], self.sems.at[0, self.index, 0])

    def load(self):
        return pltpu.make_async_copy(self.shard, self.stage, self.sems.at[0, self.index, 0])

    def push(self, offset):
        mine = pl.ds(pl.multiple_of(self.core * self.half, 16), self.half)
        return remote(self.shard.at[mine], self.full.at[self.part(self.wa, self.core)],
                      self.sems.at[1, self.index, offset - 1], self.sems.at[2, self.index, offset - 1],
                      {"wa": lax.rem(self.wa + offset, self.wa_count)})

    def hand(self, offset):
        owner = lax.rem(self.wa + self.wa_count - offset, self.wa_count)
        spot = self.full.at[self.part(owner, self.core)]
        return remote(spot, spot, self.sems.at[3, self.index, offset - 1], self.sems.at[4, self.index, offset - 1],
                      {"pln": across(self.pln, 1)})

    def begin(self):
        if self.stage is None:
            self.keep().start()
        else:
            self.load().start()
        for offset in range(1, self.wa_count):
            self.push(offset).start()

    def staged(self):
        self.load().wait()
        self.keep().start()

    def pass_on(self):
        for offset in range(1, self.wa_count):
            self.push(offset).wait_recv()
            self.hand(offset).start()

    def arrived(self):
        self.keep().wait()
        for offset in range(1, self.wa_count):
            self.hand(offset).wait_recv()

    def finish(self):
        for offset in range(1, self.wa_count):
            self.push(offset).wait_send()
            self.hand(offset).wait_send()


class Line:
    def __init__(self, full, sems, grp_count, reach, block):
        self.full, self.sems, self.count, self.reach, self.block = full, sems, grp_count, reach, block
        self.grp = lax.axis_index("grp")

    def rows(self, owner, block):
        return pl.ds(pl.multiple_of((owner * PLANE + block) * self.block, 16), self.block)

    def copy(self, side, step, block, source=None):
        toward = 1 if side == 0 else -1
        owner = self.grp - toward * (step - 1)
        spot = self.full.at[self.rows(owner, block)]
        return remote(spot if source is None else source, spot, self.sems.at[0, side, step - 1, block],
                      self.sems.at[1, side, step - 1, block], {"grp": self.grp + toward})

    def sends(self, side, step):
        if side == 0:
            return jnp.logical_and(self.grp - step + 1 >= 0, self.grp + 1 < self.count)
        return jnp.logical_and(self.grp + step - 1 < self.count, self.grp - 1 >= 0)

    def receives(self, side, step):
        return self.grp - step >= 0 if side == 0 else self.grp + step < self.count

    def send(self, step, block, source=None):
        for side in (0, 1):
            @pl.when(self.sends(side, step))
            def _():
                self.copy(side, step, block, source).start()

    def arrival(self, side, step, block):
        toward = 1 if side == 0 else -1
        spot = self.full.at[self.rows(self.grp - toward * step, block)]
        return remote(spot, spot, self.sems.at[0, side, step - 1, block], self.sems.at[1, side, step - 1, block],
                      {"grp": self.grp - toward})

    def forward(self, step):
        for block in range(PLANE):
            for side in (0, 1):
                @pl.when(self.receives(side, step))
                def _():
                    self.arrival(side, step, block).wait_recv()

                    if step < self.reach:
                        @pl.when(self.sends(side, step + 1))
                        def _():
                            self.copy(side, step + 1, block).start()

    def finish(self, source=None):
        for step in range(1, self.reach + 1):
            for block in range(PLANE):
                for side in (0, 1):
                    @pl.when(self.sends(side, step))
                    def _():
                        self.copy(side, step, block, source[block] if source and step == 1 else None).wait_send()


class Swap:
    def __init__(self, src, dst, sems):
        self.src, self.dst, self.sems = src, dst, sems
        self.pln = lax.axis_index("pln")

    def copy(self, offset):
        peer = across(self.pln, offset)
        return remote(self.src(peer), self.dst(self.pln), self.sems.at[0, offset], self.sems.at[1, offset], {"pln": peer})

    def keep(self):
        return pltpu.make_async_copy(self.src(self.pln), self.dst(self.pln), self.sems.at[0, 0])

    def begin(self):
        for offset in (2, 3, 1):
            self.copy(offset).start()
        self.keep().start()

    def arrived(self, offset):
        self.keep().wait() if offset == 0 else self.copy(offset).wait_recv()

    def finish(self):
        for offset in (1, 2, 3):
            self.copy(offset).wait_send()


def pack_vectors(refs, pack):
    pack[...] = jnp.zeros_like(pack)
    at = 0
    for ref in refs:
        length = ref.shape[0]
        width = min(128, length)
        line = ref[...].astype(jnp.float32).reshape(1, length)
        for start in range(0, length, width):
            pack[at : at + 1, :width] = line[:, start : start + width]
            at += 1


def columns_of(ref, block):
    at = pl.multiple_of(block * 128, 128)
    line = ref[0:1, pl.ds(at, 128)].astype(jnp.float32)
    return jnp.transpose(jnp.broadcast_to(line, (128, 128)))


def make_marks(lens_ref, ranks_ref, limits_ref, base, self_keys, cross_keys, self_queries, cross_queries):
    docs = lens_ref.shape[1]
    lane = lax.rem(lax.broadcasted_iota(jnp.int32, (128, 128), 1), 64)
    stat = jnp.where(jnp.logical_and(lane >= STAT, lane < STAT + 3), -1.0, 0.0)

    def document(place):
        doc, opened, total = jnp.zeros((128, 128), jnp.int32), place == 0, 0
        for d in range(docs):
            total = total + lens_ref[0, d]
            doc = doc + jnp.where(place >= total, 1, 0)
            if d < docs - 1:
                opened = jnp.logical_or(opened, place == total)
        return doc, opened

    def keys(block, _):
        place = block * 128 + lax.broadcasted_iota(jnp.int32, (128, 128), 0)
        doc, opened = document(place)
        rank = jnp.where(opened, 0, columns_of(ranks_ref, block).astype(jnp.int32) + 1)
        marks = jnp.where(lane == doc, 1.0, stat)
        there = pl.ds(pl.multiple_of(block * 128, 128), 128)
        cross_keys[there, :] = marks.astype(jnp.bfloat16)
        self_keys[there, :] = jnp.where(lane == rank + 16, 1.0, marks).astype(jnp.bfloat16)
        return 0

    def queries(block, _):
        place = base + block * 128 + lax.broadcasted_iota(jnp.int32, (128, 128), 0)
        doc, _ = document(place)
        limit = columns_of(limits_ref, base // 128 + block).astype(jnp.int32)
        marks = jnp.where(jnp.logical_and(lane < docs, lane != doc), HIDE, 0.0)
        ranks = jnp.logical_and(lane >= 16, jnp.logical_and(lane < 33, lane - 17 >= limit))
        there = pl.ds(pl.multiple_of(block * 128, 128), 128)
        cross_queries[there, :] = marks.astype(jnp.bfloat16)
        self_queries[there, :] = jnp.where(ranks, HIDE, marks).astype(jnp.bfloat16)
        return 0

    lax.fori_loop(0, self_keys.shape[0] // 128, keys, 0)
    lax.fori_loop(0, self_queries.shape[0] // 128, queries, 0)


def vector_row(pack_ref, wa_count, start, length):
    width = min(128, length)
    pieces = []
    for wa in range(wa_count):
        for row in range(length // width):
            pieces.append(pack_ref[wa, start + row : start + row + 1, :width])
    return jnp.concatenate(pieces, axis=1)


def split_pairs(value, buffer, column):
    for pair in range(PLANE):
        buffer[pair, :, column : column + 128] = value[:, pair * 128 : pair * 128 + 128]


def opening_kernel(grp_count, wa_count, reach, count, vec_at, lens_ref, ranks_ref, limits_ref, content_ref, query_ref,
                   encoder_ref, *refs):
    vecs, refs = refs[: len(vec_at)], refs[len(vec_at) :]
    shards = refs[:count]
    fulls = refs[count : 2 * count]
    vec_out, q_out, kv_out, kv2_out = refs[2 * count : 2 * count + 4]
    mark_outs = refs[2 * count + 4 : 2 * count + 8]
    marks = refs[2 * count + 8 : 2 * count + 12]
    vec_ref, held, vec_all, kvbuf, kvbuf2, qbuf, row_sems, vec_sems, line_sems, swap_sems, out_sems = refs[2 * count + 12 :]
    grp, pln, wa = lax.axis_index("grp"), lax.axis_index("pln"), lax.axis_index("wa")
    tok = content_ref.shape[0]
    gathers = [Rows(shards[i], held.at[i], row_sems, i, wa_count) for i in range(count)]
    pack_vectors(vecs, vec_ref)
    greet(grp_count, wa_count)
    vec_keep = pltpu.make_async_copy(vec_ref, vec_all.at[wa], vec_sems.at[0, 0])
    vec_keep.start()
    pushes = [remote(vec_ref, vec_all.at[wa], vec_sems.at[0, o], vec_sems.at[1, o], {"wa": lax.rem(wa + o, wa_count)})
              for o in range(1, wa_count)]
    for g in gathers[:2]:
        g.begin()
    for p in pushes:
        p.start()
    for g in gathers[:2]:
        g.pass_on()
    for g in gathers[2:5]:
        g.begin()
    vec_keep.wait()
    for p in pushes:
        p.wait_recv()
    for g in gathers[:2]:
        g.arrived()
    content = content_ref[...]
    split_pairs(matmul(content, held[0]).astype(jnp.bfloat16), kvbuf, 0)
    row = lambda i: vector_row(vec_all, wa_count, *vec_at[i])
    split_pairs((matmul(content, held[1]) + row(1)).astype(jnp.bfloat16), kvbuf, 128)
    line = Line(kv_out, line_sems, grp_count, reach, tok)
    spot = lambda ref: lambda p: ref.at[pl.ds(pl.multiple_of((grp * PLANE + p) * tok, 16), tok)]
    swap = Swap(lambda p: kvbuf.at[p], spot(kv_out), swap_sems.at[0])
    swap.begin()
    line.send(1, pln, kvbuf.at[pln])
    swap.arrived(1)
    line.send(1, across(pln, 1))
    for g in gathers[2:5]:
        g.pass_on()
    for g in gathers[5:]:
        g.begin()
    for offset in (2, 3):
        swap.arrived(offset)
        line.send(1, across(pln, offset))
    for g in gathers[2:5]:
        g.arrived()
    outs = [pltpu.make_async_copy(held.at[i], fulls[i], out_sems.at[i]) for i in range(count)]
    for o in outs[:5]:
        o.start()
    vec_save = pltpu.make_async_copy(vec_all, vec_out, out_sems.at[count])
    vec_save.start()
    query = (matmul(query_ref[...], held[2]) + row(0)).astype(jnp.bfloat16)
    query = query * 0.125
    for pair in range(PLANE):
        qbuf[pair] = query[:, pair * 128 : pair * 128 + 128]
    place = lambda p: q_out.at[pl.ds(pl.multiple_of(p * tok, 16), tok)]
    swap_q = Swap(lambda p: qbuf.at[p], place, swap_sems.at[1])
    swap_q.begin()
    encoder = encoder_ref[...]
    split_pairs(matmul(encoder, held[3]).astype(jnp.bfloat16), kvbuf2, 0)
    split_pairs((matmul(encoder, held[4]) + row(2)).astype(jnp.bfloat16), kvbuf2, 128)
    place2 = lambda p: kv2_out.at[pl.ds(pl.multiple_of(p * tok, 16), tok)]
    swap_2 = Swap(lambda p: kvbuf2.at[p], place2, swap_sems.at[2])
    swap_2.begin()
    make_marks(lens_ref, ranks_ref, limits_ref, grp * PLANE * tok, *marks)
    mark_saves = [pltpu.make_async_copy(m, o, out_sems.at[count + 1 + i]) for i, (m, o) in enumerate(zip(marks, mark_outs))]
    for m in mark_saves:
        m.start()
    for step in range(1, reach + 1):
        line.forward(step)
    swap.arrived(0)
    for s in (swap_q, swap_2):
        for offset in range(4):
            s.arrived(offset)
    for g in gathers[5:]:
        g.pass_on()
    for g in gathers[5:]:
        g.arrived()
    for o in outs[5:]:
        o.start()
    for g in gathers:
        g.finish()
    for p in pushes:
        p.wait_send()
    for o in outs:
        o.wait()
    vec_save.wait()
    for m in mark_saves:
        m.wait()
    line.finish()
    for s in (swap, swap_q, swap_2):
        s.finish()


def run_opening(grp_count, wa_count, lens, ranks, limits, content, query, encoder, vecs, mats, vec_at):
    tok = content.shape[0]
    reach = min(grp_count - 1, (DOCLEN + PLANE * tok - 2) // (PLANE * tok))
    count = len(mats)
    low = jnp.bfloat16
    shape = lambda *s: jax.ShapeDtypeStruct(s, low)
    out_shape = [shape(m.shape[0] * wa_count, m.shape[1]) for m in mats]
    rows, keys = PLANE * tok, grp_count * PLANE * tok
    used = sum(length // min(128, length) for _, length in vec_at)
    pack = (used + -used % 16, 128)
    marks = [(keys, 128), (keys, 128), (rows, 128), (rows, 128)]
    out_shape += [jax.ShapeDtypeStruct((wa_count,) + pack, jnp.float32), shape(rows, 128), shape(keys, 256), shape(rows, 256)]
    out_shape += [shape(*m) for m in marks]
    return pl.pallas_call(
        functools.partial(opening_kernel, grp_count, wa_count, reach, count, vec_at),
        out_shape=tuple(out_shape),
        in_specs=[SMEM] + [VMEM] * (5 + len(vecs)) + [ANY] * count,
        out_specs=tuple([ANY] * len(out_shape)),
        scratch_shapes=[pltpu.VMEM(m, low) for m in marks] + [
            pltpu.VMEM(pack, jnp.float32), pltpu.VMEM((count, 512, 512), low), pltpu.VMEM((wa_count,) + pack, jnp.float32),
            pltpu.VMEM((PLANE, tok, 256), low), pltpu.VMEM((PLANE, tok, 256), low), pltpu.VMEM((PLANE, tok, 128), low),
            DMA((5, count, max(1, wa_count - 1))), DMA((2, wa_count)), DMA((2, 2, reach, PLANE)), DMA((3, 2, 4)),
            DMA((count + 5,))],
        cost_estimate=pl.CostEstimate(flops=38000000000, bytes_accessed=0, transcendentals=0),
        compiler_params=pltpu.CompilerParams(collective_id=1, has_side_effects=True, vmem_limit_bytes=60 << 20),
    )(lens, ranks, limits, content, query, encoder, *vecs, *mats)


def flat_pairs(buffer):
    return jnp.concatenate([buffer[p] for p in range(PLANE)], axis=1)


def middle_kernel(grp_count, wa_count, reach, vec_at, attended_ref, query_ref, out_mat_ref, query_mat_ref, vec_ref,
                  kv_own_ref, expand_ref, shrink_ref,
                  hidden_ref, normed_ref, inverse_ref, mixed_ref, q_out, kv_out, expand_full, shrink_full,
                  sendbuf, mixbuf, qbuf, expand_stage, shrink_stage, kv_stage, row_sems, line_sems, swap_sems, keep_sem):
    grp, pln = lax.axis_index("grp"), lax.axis_index("pln")
    tok = query_ref.shape[0]
    gathers = [Rows(expand_ref, expand_full, row_sems, 0, wa_count, expand_stage),
               Rows(shrink_ref, shrink_full, row_sems, 1, wa_count, shrink_stage)]
    load = pltpu.make_async_copy(kv_own_ref, kv_stage, keep_sem)
    load.start()
    for p in range(PLANE):
        sendbuf[p] = attended_ref[p * tok : p * tok + tok, :].astype(jnp.bfloat16)
    greet(grp_count, wa_count)
    swap = Swap(lambda p: sendbuf.at[p], lambda p: mixbuf.at[p], swap_sems.at[0])
    swap.begin()
    line = Line(kv_out, line_sems, grp_count, reach, tok)
    sources = [kv_own_ref.at[pl.ds(b * tok, tok)] for b in range(PLANE)]
    for b in range(PLANE):
        line.send(1, b, sources[b])
    for g in gathers:
        g.begin()
    whole = pl.ds(pl.multiple_of(grp * PLANE * tok, 16), PLANE * tok)
    load.wait()
    keep = pltpu.make_async_copy(kv_stage, kv_out.at[whole], keep_sem)
    keep.start()
    row = lambda i: vector_row(vec_ref, wa_count, *vec_at[i])
    for offset in range(4):
        swap.arrived(offset)
    mixed = flat_pairs(mixbuf)
    mixed_ref[...] = mixed
    value = query_ref[...].astype(jnp.float32) + matmul(mixed, out_mat_ref[...]) + row(3)
    hidden, normed, inverse = norm_forward(value, row(4), row(5))
    hidden_ref[...] = hidden
    normed_ref[...] = normed
    inverse_ref[...] = jnp.broadcast_to(inverse, inverse_ref.shape)
    query = (matmul(hidden.astype(jnp.bfloat16), query_mat_ref[...]) + row(6)).astype(jnp.bfloat16) * 0.125
    for pair in range(PLANE):
        qbuf[pair] = query[:, pair * 128 : pair * 128 + 128]
    place = lambda p: q_out.at[pl.ds(pl.multiple_of(p * tok, 16), tok)]
    swap_q = Swap(lambda p: qbuf.at[p], place, swap_sems.at[1])
    swap_q.begin()
    for g in gathers:
        g.staged()
    line.forward(1)
    for g in gathers:
        g.pass_on()
    for step in range(2, reach + 1):
        line.forward(step)
    for offset in range(4):
        swap_q.arrived(offset)
    for g in gathers:
        g.arrived()
    for g in gathers:
        g.finish()
    line.finish(sources)
    keep.wait()
    swap.finish()
    swap_q.finish()


def run_middle(grp_count, wa_count, attended, query, out_mat, query_mat, vecs, vec_at, kv_own, expand, shrink):
    tok = query.shape[0]
    reach = min(grp_count - 1, (DOCLEN + PLANE * tok - 2) // (PLANE * tok))
    low, full = jnp.bfloat16, jnp.float32
    shape = jax.ShapeDtypeStruct
    return pl.pallas_call(
        functools.partial(middle_kernel, grp_count, wa_count, reach, vec_at),
        out_shape=(shape((tok, 512), full), shape((tok, 512), full), shape((tok, 128), full), shape((tok, 512), low),
                   shape((PLANE * tok, 128), low), shape((grp_count * PLANE * tok, 256), low),
                   shape((expand.shape[0] * wa_count, expand.shape[1]), low),
                   shape((shrink.shape[0] * wa_count, shrink.shape[1]), low)),
        in_specs=[VMEM] * 5 + [ANY] * 3,
        out_specs=tuple([VMEM] * 4 + [ANY] * 4),
        scratch_shapes=[
            pltpu.VMEM((PLANE, tok, 128), low), pltpu.VMEM((PLANE, tok, 128), low), pltpu.VMEM((PLANE, tok, 128), low),
            pltpu.VMEM(expand.shape, low), pltpu.VMEM(shrink.shape, low), pltpu.VMEM((PLANE * tok, 256), low),
            DMA((5, 2, max(1, wa_count - 1))), DMA((2, 2, reach, PLANE)), DMA((2, 2, 4)), DMA],
        cost_estimate=pl.CostEstimate(flops=30000000000, bytes_accessed=0, transcendentals=0),
        compiler_params=pltpu.CompilerParams(collective_id=2, has_side_effects=True, vmem_limit_bytes=60 << 20),
    )(attended, query, out_mat, query_mat, vecs, kv_own, expand, shrink)


def swap_kernel(inverse, in_ref, out_ref, sendbuf, getbuf, swap_sems):
    tok = getbuf.shape[1]
    for p in range(PLANE):
        if inverse:
            sendbuf[p] = in_ref[p * tok : p * tok + tok, :].astype(jnp.bfloat16)
        else:
            sendbuf[p] = in_ref[:, p * 128 : p * 128 + 128].astype(jnp.bfloat16)
    greet(1, 1, groups=False, rows=False)
    swap = Swap(lambda p: sendbuf.at[p], lambda p: getbuf.at[p], swap_sems)
    swap.begin()
    for offset in range(4):
        swap.arrived(offset)
    for p in range(PLANE):
        if inverse:
            out_ref[:, p * 128 : p * 128 + 128] = getbuf[p]
        else:
            out_ref[p * tok : p * tok + tok, :] = getbuf[p]
    swap.finish()


def run_swap(inverse, value, ident):
    tok = value.shape[0] // PLANE if inverse else value.shape[0]
    low = jnp.bfloat16
    return pl.pallas_call(
        functools.partial(swap_kernel, inverse),
        out_shape=jax.ShapeDtypeStruct((tok, 512) if inverse else (PLANE * tok, 128), low),
        in_specs=[VMEM], out_specs=VMEM,
        scratch_shapes=[pltpu.VMEM((PLANE, tok, 128), low), pltpu.VMEM((PLANE, tok, 128), low), DMA((2, 4))],
        cost_estimate=pl.CostEstimate(flops=6000000000, bytes_accessed=0, transcendentals=0),
        compiler_params=pltpu.CompilerParams(collective_id=ident, has_side_effects=True, vmem_limit_bytes=60 << 20),
    )(value)


class Fold:
    def __init__(self, partial, mine, sendbuf, getbuf, sems, load_sems, grp_count, reach, block):
        self.partial, self.mine, self.sendbuf, self.getbuf = partial, mine, sendbuf, getbuf
        self.sems, self.load_sems = sems, load_sems
        self.count, self.reach, self.block = grp_count, reach, block
        self.grp = lax.axis_index("grp")

    def toward(self, side):
        return 1 if side == 0 else -1

    def rows(self, owner, block):
        return pl.ds(pl.multiple_of((owner * PLANE + block) * self.block, 16), self.block)

    def part(self, block):
        return pl.ds(block * self.block, self.block)

    def sends(self, side, stage):
        return self.grp + stage < self.count if side == 0 else self.grp - stage >= 0

    def receives(self, side, stage):
        if side == 0:
            return jnp.logical_and(self.grp >= 1, self.grp - 1 + stage < self.count)
        return jnp.logical_and(self.grp + 1 < self.count, self.grp + 1 - stage >= 0)

    def copy(self, side, stage, block, back=False):
        source = self.sendbuf.at[side, stage - 1, self.part(block)]
        if stage == self.reach and not back:
            source = self.partial.at[self.rows(self.grp + self.toward(side) * stage, block)]
        peer = self.grp + (-self.toward(side) if back else self.toward(side))
        return remote(source, self.getbuf.at[side, stage - 1, self.part(block)], self.sems.at[0, side, stage - 1, block],
                      self.sems.at[1, side, stage - 1, block], {"grp": peer})

    def load(self, side, stage):
        size = PLANE * self.block
        rows = pl.ds(pl.multiple_of((self.grp + self.toward(side) * stage) * size, 16), size)
        return pltpu.make_async_copy(self.partial.at[rows], self.mine.at[side, stage - 1], self.load_sems.at[side, stage - 1])

    def begin(self):
        for block in range(PLANE):
            for side in (0, 1):
                @pl.when(self.sends(side, self.reach))
                def _():
                    self.copy(side, self.reach, block).start()
        for stage in range(1, self.reach):
            for side in (0, 1):
                @pl.when(self.sends(side, stage))
                def _():
                    self.load(side, stage).start()

    def grow(self, stage):
        for side in (0, 1):
            @pl.when(self.sends(side, stage))
            def _():
                self.load(side, stage).wait()
        for block in range(PLANE):
            part = self.part(block)
            for side in (0, 1):
                @pl.when(self.sends(side, stage))
                def _():
                    self.sendbuf[side, stage - 1, part, :] = self.mine[side, stage - 1, part, :]

                    @pl.when(self.receives(side, stage + 1))
                    def _():
                        self.copy(side, stage + 1, block, True).wait_recv()
                        total = self.mine[side, stage - 1, part, :].astype(jnp.float32)
                        total = total + self.getbuf[side, stage, part, :].astype(jnp.float32)
                        self.sendbuf[side, stage - 1, part, :] = total.astype(jnp.bfloat16)

                    self.copy(side, stage, block).start()

    def total(self, own, out):
        for block in range(PLANE):
            part = self.part(block)
            for side in (0, 1):
                @pl.when(self.receives(side, 1))
                def _():
                    self.copy(side, 1, block, True).wait_recv()
                    own[part, :] = own[part, :] + self.getbuf[side, 0, part, :].astype(jnp.float32)
            out[block] = own[part, :].astype(jnp.bfloat16)

    def finish(self):
        for stage in range(1, self.reach + 1):
            for block in range(PLANE):
                for side in (0, 1):
                    @pl.when(self.sends(side, stage))
                    def _():
                        self.copy(side, stage, block, True).wait_send()


def store_blocks(buffer, value):
    for c in range(PLANE):
        buffer[c] = value[:, c * 128 : c * 128 + 128].astype(jnp.bfloat16)


def halves(buffer):
    keys = jnp.concatenate([buffer[p, :, :128] for p in range(PLANE)], axis=1)
    values = jnp.concatenate([buffer[p, :, 128:] for p in range(PLANE)], axis=1)
    return keys, values


def turn_kernel(grp_count, wa_count, reach, vec_at, dq_ref, dkv_ref, own_ref, back_ref, normed_ref, inverse_ref, hidden_ref,
                mixed_one_ref, mixed_two_ref, branch_two_ref, encoder_ref, query_mat_ref, out_mat_ref, vec_ref, vg_ref,
                do_out, back_out, kv_out, grads_out, vg_out,
                dqsend, dqget, dosend, doget, kvsend, kvget, total, mine, foldsend, foldget, grads, fold_sems, load_sems,
                swap_sems, out_sems):
    tok = back_ref.shape[0]
    for p in range(PLANE):
        dqsend[p] = dq_ref[p * tok : p * tok + tok, :]
    greet(grp_count, wa_count, rows=False)
    swap_dq = Swap(lambda p: dqsend.at[p], lambda p: dqget.at[p], swap_sems.at[0])
    swap_dq.begin()
    fold = Fold(dkv_ref, mine, foldsend, foldget, fold_sems, load_sems, grp_count, reach, tok)
    fold.begin()
    row = lambda i: vector_row(vec_ref, wa_count, *vec_at[i])
    vg_out[...] = vg_ref[...]
    saves = [pltpu.make_async_copy(grads.at[i], grads_out.at[i], out_sems.at[i]) for i in range(5)]
    total[...] = own_ref[...]
    store_blocks(grads.at[0], dot(mixed_two_ref[...], branch_two_ref[...], 0, 0))
    saves[0].start()
    for offset in range(4):
        swap_dq.arrived(offset)
    dq = flat_pairs(dqget)
    incoming = back_ref[...] + dot(dq, query_mat_ref[...], 1, 1)
    back, gain_grad, shift_grad = norm_backward(incoming, normed_ref[...], inverse_ref[:, :1], row(4))
    back_out[...] = back
    branch = back.astype(jnp.bfloat16)
    do = dot(branch, out_mat_ref[...], 1, 1).astype(jnp.bfloat16)
    for p in range(PLANE):
        dosend[p] = do[:, p * 128 : p * 128 + 128]
    swap_do = Swap(lambda p: dosend.at[p], lambda p: doget.at[p], swap_sems.at[1])
    swap_do.begin()
    vg_out[10:11, :] = gain_grad.reshape(1, 512)
    vg_out[11:12, :] = shift_grad.reshape(1, 512)
    vg_out[12:13, :] = column_sum(branch).reshape(1, 512)
    vg_out[13:14, :] = column_sum(dq).reshape(1, 512)
    store_blocks(grads.at[1], dot(hidden_ref[...].astype(jnp.bfloat16), dq, 0, 0))
    saves[1].start()
    store_blocks(grads.at[2], dot(mixed_one_ref[...], branch, 0, 0))
    saves[2].start()
    for stage in range(reach - 1, 0, -1):
        fold.grow(stage)
    for offset in range(4):
        swap_do.arrived(offset)
    for p in range(PLANE):
        do_out[p * tok : p * tok + tok, :] = doget[p]
    fold.total(total, kvsend)
    swap_kv = Swap(lambda p: kvsend.at[p], lambda p: kvget.at[p], swap_sems.at[2])
    swap_kv.begin()
    for offset in range(4):
        swap_kv.arrived(offset)
    keys, values = halves(kvget)
    kv_out[:, :512] = keys
    kv_out[:, 512:] = values
    encoder = encoder_ref[...]
    store_blocks(grads.at[3], dot(encoder, keys, 0, 0))
    saves[3].start()
    store_blocks(grads.at[4], dot(encoder, values, 0, 0))
    saves[4].start()
    vg_out[14:15, :] = column_sum(values).reshape(1, 512)
    for s in saves:
        s.wait()
    fold.finish()
    for s in (swap_dq, swap_do, swap_kv):
        s.finish()


def fold_scratch(tok, reach):
    low = jnp.bfloat16
    size = PLANE * tok
    return [pltpu.VMEM((PLANE, tok, 256), low), pltpu.VMEM((PLANE, tok, 256), low), pltpu.VMEM((size, 256), jnp.float32),
            pltpu.VMEM((2, max(1, reach - 1), size, 256), low), pltpu.VMEM((2, reach, size, 256), low),
            pltpu.VMEM((2, reach, size, 256), low)]


def run_turn(grp_count, wa_count, vec_at, dq, dkv, own, back, normed, inverse, hidden, mixed_one, mixed_two, branch_two,
             encoder, query_mat, out_mat, vecs, vg):
    tok = back.shape[0]
    reach = min(grp_count - 1, (DOCLEN + PLANE * tok - 2) // (PLANE * tok))
    low, full = jnp.bfloat16, jnp.float32
    shape = jax.ShapeDtypeStruct
    pairs = pltpu.VMEM((PLANE, tok, 128), low)
    return pl.pallas_call(
        functools.partial(turn_kernel, grp_count, wa_count, reach, vec_at),
        out_shape=(shape((PLANE * tok, 128), low), shape((tok, 512), full), shape((tok, 1024), low),
                   shape((5, PLANE, 512, 128), low), shape(vg.shape, full)),
        in_specs=[VMEM, ANY] + [VMEM] * 13,
        out_specs=(VMEM, VMEM, VMEM, ANY, VMEM),
        scratch_shapes=[pairs] * 4 + fold_scratch(tok, reach) + [
            pltpu.VMEM((5, PLANE, 512, 128), low), DMA((2, 2, reach, PLANE)), DMA((2, max(1, reach - 1))), DMA((3, 2, 4)),
            DMA((5,))],
        cost_estimate=pl.CostEstimate(flops=32000000000, bytes_accessed=0, transcendentals=0),
        compiler_params=pltpu.CompilerParams(collective_id=8, has_side_effects=True, vmem_limit_bytes=60 << 20),
    )(dq, dkv, own, back, normed, inverse, hidden, mixed_one, mixed_two, branch_two, encoder, query_mat, out_mat, vecs, vg)


class Reduce:
    def __init__(self, index, source, parts, got, kept, sems, wa_count):
        self.index, self.source, self.sems, self.wa_count = index, source, sems, wa_count
        self.parts, (self.got_core, self.got_wa, self.got_row) = parts, got
        self.by_core, self.by_wa, self.by_row = kept
        self.wa, self.pln = lax.axis_index("wa"), lax.axis_index("pln")
        self.core = lax.rem(self.pln, 2)
        self.row = self.pln // 2
        self.size = 512 // wa_count

    def core_copy(self, row):
        return remote(self.source.at[row * 2 + 1 - self.core], self.got_core.at[self.index, row],
                      self.sems.at[0, self.index, row], self.sems.at[1, self.index, row], {"pln": across(self.pln, 1)})

    def rows_of(self, wa):
        return pl.ds(pl.multiple_of(wa * self.size, 16), self.size)

    def wa_copy(self, offset):
        peer = lax.rem(self.wa + offset, self.wa_count)
        return remote(self.by_core.at[self.index, :, self.rows_of(peer)], self.got_wa.at[offset - 1, self.index],
                      self.sems.at[0, self.index, 1 + offset], self.sems.at[1, self.index, 1 + offset], {"wa": peer})

    def row_copy(self):
        return remote(self.by_wa.at[self.index, 1 - self.row], self.got_row.at[self.index],
                      self.sems.at[0, self.index, 1 + self.wa_count], self.sems.at[1, self.index, 1 + self.wa_count],
                      {"pln": across(self.pln, 2)})

    def begin(self):
        for row in (0, 1):
            self.core_copy(row).start()

    def after_core(self):
        for row in (0, 1):
            self.core_copy(row).wait_recv()
            mine = self.parts[row * 2 + self.core].astype(jnp.float32)
            total = mine + self.got_core[self.index, row].astype(jnp.float32)
            self.by_core[self.index, row] = total.astype(jnp.bfloat16)
        for offset in range(1, self.wa_count):
            self.wa_copy(offset).start()

    def after_wa(self):
        for offset in range(1, self.wa_count):
            self.wa_copy(offset).wait_recv()
        for row in (0, 1):
            total = self.by_core[self.index, row, self.rows_of(self.wa), :].astype(jnp.float32)
            for offset in range(1, self.wa_count):
                total = total + self.got_wa[offset - 1, self.index, row].astype(jnp.float32)
            self.by_wa[self.index, row] = total.astype(jnp.bfloat16)
        self.row_copy().start()

    def after_row(self):
        self.row_copy().wait_recv()
        total = self.by_wa[self.index, self.row].astype(jnp.float32) + self.got_row[self.index].astype(jnp.float32)
        self.by_row[self.index] = total.astype(jnp.bfloat16)

    def finish(self):
        for row in (0, 1):
            self.core_copy(row).wait_send()
        for offset in range(1, self.wa_count):
            self.wa_copy(offset).wait_send()
        self.row_copy().wait_send()


def greet_all(grp_count, wa_count):
    barrier = pltpu.get_barrier_semaphore()
    grp, pln, wa = lax.axis_index("grp"), lax.axis_index("pln"), lax.axis_index("wa")
    peers = [{"pln": across(pln, o)} for o in (1, 2, 3)]
    peers += [{"wa": lax.rem(wa + o, wa_count)} for o in range(1, wa_count)]
    peers += [{"grp": lax.rem(grp + o, grp_count)} for o in range(1, grp_count)]
    for where in peers:
        pl.semaphore_signal(barrier, inc=1, device_id=where, device_id_type=MESH)
    pl.semaphore_wait(barrier, len(peers))


def closing_kernel(grp_count, wa_count, reach, count, dq_ref, dkv_ref, own_ref, query_ref, content_ref, early_ref, vg_ref,
                   dq_out, kv_out, out_ref, vg_out,
                   dqsend, dqget, kvsend, kvget, total, mine, foldsend, foldget, parts, got_core, got_wa, got_row,
                   by_core, by_wa, by_row, got_grp, final, vsum, vgot, vall,
                   fold_sems, load_sems, swap_sems, part_sems, red_sems, vec_sems, grp_sems, share_sems):
    grp, pln, wa = lax.axis_index("grp"), lax.axis_index("pln"), lax.axis_index("wa")
    tok = query_ref.shape[0]
    early = early_ref.shape[0]
    size = 512 // wa_count
    slab = size // grp_count
    for p in range(PLANE):
        dqsend[p] = dq_ref[p * tok : p * tok + tok, :]
    greet_all(grp_count, wa_count)
    swap_dq = Swap(lambda p: dqsend.at[p], lambda p: dqget.at[p], swap_sems.at[0])
    swap_dq.begin()
    fold = Fold(dkv_ref, mine, foldsend, foldget, fold_sems, load_sems, grp_count, reach, tok)
    fold.begin()
    loads = [pltpu.make_async_copy(early_ref.at[i], parts.at[i], part_sems.at[i]) for i in range(early)]
    for l in loads:
        l.start()
    got, kept = (got_core, got_wa, got_row), (by_core, by_wa, by_row)
    reds = [Reduce(i, early_ref.at[i] if i < early else parts.at[i], parts.at[i], got, kept, red_sems, wa_count)
            for i in range(count)]
    for r in reds[:early]:
        r.begin()
    total[...] = own_ref[...]
    vsum[0] = vg_ref[...]
    for offset in range(4):
        swap_dq.arrived(offset)
    dq = flat_pairs(dqget)
    dq_out[...] = dq
    store_blocks(parts.at[early], dot(query_ref[...], dq, 0, 0))
    vsum[0, 15:16, :] = column_sum(dq).reshape(1, 512)
    reds[early].begin()
    for l in loads:
        l.wait()
    for r in reds[: early + 1]:
        r.after_core()
    for stage in range(reach - 1, 0, -1):
        fold.grow(stage)
    for r in reds[: early + 1]:
        r.after_wa()
    fold.total(total, kvsend)
    swap_kv = Swap(lambda p: kvsend.at[p], lambda p: kvget.at[p], swap_sems.at[1])
    swap_kv.begin()
    for r in reds[: early + 1]:
        r.after_row()
    for offset in range(4):
        swap_kv.arrived(offset)
    keys, values = halves(kvget)
    content = content_ref[...]
    store_blocks(parts.at[early + 1], dot(content, keys, 0, 0))
    reds[early + 1].begin()
    store_blocks(parts.at[early + 2], dot(content, values, 0, 0))
    reds[early + 2].begin()
    vsum[0, 16:17, :] = column_sum(values).reshape(1, 512)
    vec_core = remote(vsum.at[0], vgot.at[0], vec_sems.at[0, 0], vec_sems.at[1, 0], {"pln": across(pln, 1)})
    vec_core.start()
    kv_out[:, :512] = keys
    kv_out[:, 512:] = values

    def grp_copy(set_at, offset):
        start, length = ((0, early + 1), (early + 1, count - early - 1))[set_at]
        peer = lax.rem(grp + offset, grp_count)
        some = pl.ds(start, length)
        rows = pl.ds(pl.multiple_of(peer * slab, 8), slab)
        return remote(by_row.at[some, rows], got_grp.at[offset - 1, some], grp_sems.at[0, set_at, offset - 1],
                      grp_sems.at[1, set_at, offset - 1], {"grp": peer})

    offsets = range(1, grp_count)
    for o in offsets:
        grp_copy(0, o).start()
    for r in reds[early + 1 :]:
        r.after_core()
    vec_core.wait_recv()
    vsum[1] = vsum[0] + vgot[0]
    vec_wa = [remote(vsum.at[1], vgot.at[o], vec_sems.at[0, o], vec_sems.at[1, o], {"wa": lax.rem(wa + o, wa_count)})
              for o in range(1, wa_count)]
    for v in vec_wa:
        v.start()
    for r in reds[early + 1 :]:
        r.after_wa()
    for v in vec_wa:
        v.wait_recv()
    vall[wa] = vsum[1]
    for o in range(1, wa_count):
        vall[lax.rem(wa + wa_count - o, wa_count)] = vgot[o]
    joined = vall[0]
    for o in range(1, wa_count):
        joined = joined + vall[o]
    vsum[2] = joined
    vec_row = remote(vsum.at[2], vgot.at[wa_count], vec_sems.at[0, wa_count], vec_sems.at[1, wa_count],
                     {"pln": across(pln, 2)})
    vec_row.start()
    own_rows = pl.ds(pl.multiple_of(grp * slab, 8), slab)

    def settle(set_at):
        start, length = ((0, early + 1), (early + 1, count - early - 1))[set_at]
        some = pl.ds(start, length)
        for o in offsets:
            grp_copy(set_at, o).wait_recv()
        value = by_row[some, own_rows, :].astype(jnp.float32)
        for o in offsets:
            value = value + got_grp[o - 1, some].astype(jnp.float32)
        final[some] = value.astype(jnp.bfloat16)

    def spot(column, source, some):
        return out_ref.at[column, some, pl.ds(pl.multiple_of(source * slab, 8), slab)]

    def spread(set_at, offset):
        start, length = ((0, early + 1), (early + 1, count - early - 1))[set_at]
        some = pl.ds(start, length)
        return remote(final.at[some], spot(pln, grp, some), share_sems.at[0, set_at, 0, offset],
                      share_sems.at[1, set_at, 0, offset], {"grp": lax.rem(grp + offset, grp_count)})

    def keep(set_at):
        start, length = ((0, early + 1), (early + 1, count - early - 1))[set_at]
        some = pl.ds(start, length)
        return pltpu.make_async_copy(final.at[some], spot(pln, grp, some), share_sems.at[0, set_at, 0, 0])

    def give(set_at, kind, offset):
        start, length = ((0, early + 1), (early + 1, count - early - 1))[set_at]
        some = pl.ds(start, length)
        source = lax.rem(grp + grp_count - offset, grp_count)
        column = pln if kind < 3 else across(pln, 2)
        there = spot(column, source, some)
        return remote(there, there, share_sems.at[0, set_at, kind, offset], share_sems.at[1, set_at, kind, offset],
                      {"pln": across(pln, 2 if kind == 1 else 1)})

    settle(0)
    keep(0).start()
    for o in offsets:
        spread(0, o).start()
    for r in reds[early + 1 :]:
        r.after_row()
    for o in offsets:
        grp_copy(1, o).start()
    vec_row.wait_recv()
    vsum[3] = vsum[2] + vgot[wa_count]
    vec_grp = [remote(vsum.at[3], vall.at[wa_count + o], vec_sems.at[0, wa_count + o], vec_sems.at[1, wa_count + o],
                      {"grp": lax.rem(grp + o, grp_count)}) for o in offsets]
    for v in vec_grp:
        v.start()
    everyone = range(grp_count)

    def hand_out(set_at, offset):
        if offset == 0:
            keep(set_at).wait()
        else:
            spread(set_at, offset).wait_recv()
        give(set_at, 1, offset).start()
        give(set_at, 2, offset).start()

    for o in everyone:
        hand_out(0, o)
    settle(1)
    keep(1).start()
    for o in offsets:
        spread(1, o).start()
    for o in everyone:
        give(0, 1, o).wait_recv()
        give(0, 3, o).start()
    for o in everyone:
        hand_out(1, o)
    for v in vec_grp:
        v.wait_recv()
    ordered = jnp.zeros_like(vsum[3])
    for g in everyone:
        piece = jnp.where(grp == g, vsum[3], 0.0)
        for o in offsets:
            piece = piece + jnp.where(lax.rem(grp + grp_count - o, grp_count) == g, vall[wa_count + o], 0.0)
        ordered = ordered + piece
    vg_out[...] = ordered
    for o in everyone:
        give(1, 1, o).wait_recv()
        give(1, 3, o).start()
    for set_at in (0, 1):
        for o in everyone:
            give(set_at, 2, o).wait_recv()
            give(set_at, 3, o).wait_recv()
    for set_at in (0, 1):
        for o in everyone:
            for kind in (1, 2, 3):
                give(set_at, kind, o).wait_send()
        for o in offsets:
            spread(set_at, o).wait_send()
            grp_copy(set_at, o).wait_send()
    for v in [vec_core, vec_row] + vec_wa + vec_grp:
        v.wait_send()
    for r in reds:
        r.finish()
    fold.finish()
    swap_dq.finish()
    swap_kv.finish()


def run_closing(grp_count, wa_count, dq, dkv, own, query, content, early, vg):
    tok = query.shape[0]
    count = early.shape[0] + 3
    reach = min(grp_count - 1, (DOCLEN + PLANE * tok - 2) // (PLANE * tok))
    size = 512 // wa_count
    slab = size // grp_count
    low, full = jnp.bfloat16, jnp.float32
    shape = jax.ShapeDtypeStruct
    pairs = pltpu.VMEM((PLANE, tok, 128), low)
    steps = wa_count + 2
    return pl.pallas_call(
        functools.partial(closing_kernel, grp_count, wa_count, reach, count),
        out_shape=(shape((tok, 512), low), shape((tok, 1024), low), shape((PLANE, count, size, 128), low),
                   shape(vg.shape, full)),
        in_specs=[VMEM, ANY, VMEM, VMEM, VMEM, ANY, VMEM],
        out_specs=(VMEM, VMEM, ANY, VMEM),
        scratch_shapes=[pairs] * 2 + fold_scratch(tok, reach) + [
            pltpu.VMEM((count, PLANE, 512, 128), low), pltpu.VMEM((count, 2, 512, 128), low),
            pltpu.VMEM((max(1, wa_count - 1), count, 2, size, 128), low), pltpu.VMEM((count, size, 128), low),
            pltpu.VMEM((count, 2, 512, 128), low), pltpu.VMEM((count, 2, size, 128), low), pltpu.VMEM((count, size, 128), low),
            pltpu.VMEM((grp_count - 1, count, slab, 128), low), pltpu.VMEM((count, slab, 128), low),
            pltpu.VMEM((4,) + vg.shape, full), pltpu.VMEM((wa_count + 1,) + vg.shape, full),
            pltpu.VMEM((wa_count + grp_count,) + vg.shape, full),
            DMA((2, 2, reach, PLANE)), DMA((2, max(1, reach - 1))), DMA((2, 2, 4)), DMA((early.shape[0],)),
            DMA((2, count, steps)), DMA((2, wa_count + grp_count)), DMA((2, 2, grp_count - 1)), DMA((2, 2, 4, grp_count))],
        cost_estimate=pl.CostEstimate(flops=75000000000, bytes_accessed=0, transcendentals=0),
        compiler_params=pltpu.CompilerParams(collective_id=9, has_side_effects=True, vmem_limit_bytes=60 << 20),
    )(dq, dkv, own, query, content, early, vg)


def centre_kernel(wa_count, vec_at, attended_ref, hidden_ref, cotangent_ref, out_mat_ref, expand_ref, shrink_ref, vec_ref,
                  layer_out, mixed_out, back_out, branch_out, do_out, grad_shrink, grad_expand, vg_out,
                  sendbuf, getbuf, dosend, doget, slopes, actives, swap_sems):
    tok = hidden_ref.shape[0]
    for p in range(PLANE):
        sendbuf[p] = attended_ref[p * tok : p * tok + tok, :].astype(jnp.bfloat16)
    greet(1, 1, groups=False, rows=False)
    swap = Swap(lambda p: sendbuf.at[p], lambda p: getbuf.at[p], swap_sems.at[0])
    swap.begin()
    row = lambda i: vector_row(vec_ref, wa_count, *vec_at[i])
    vg_out[...] = jnp.zeros_like(vg_out)
    for offset in range(4):
        swap.arrived(offset)
    mixed = flat_pairs(getbuf)
    mixed_out[...] = mixed
    value = hidden_ref[...] + matmul(mixed, out_mat_ref[...]) + row(7)
    hidden, normed_two, inverse_two = norm_forward(value, row(8), row(9))
    low = hidden.astype(jnp.bfloat16)
    expand_row = row(10)
    total = hidden + row(11)
    width = 512
    chunks = expand_ref.shape[1] // width
    for c in range(chunks):
        span = slice(c * width, c * width + width)
        u = matmul(low, expand_ref[:, span]) + expand_row[:, span]
        cumulative = 0.5 * (1.0 + lax.erf(u * ROOT_HALF))
        active = (u * cumulative).astype(jnp.bfloat16)
        actives[:, span] = active
        slopes[:, span] = cumulative + u * jnp.exp(-0.5 * u * u) * INV_ROOT_TWO_PI
        total = total + matmul(active, shrink_ref[span, :])
    out, normed_three, inverse_three = norm_forward(total, row(12), row(13))
    layer_out[...] = out
    cotangent = cotangent_ref[...].astype(jnp.float32)
    back, gain_grad, shift_grad = norm_backward(cotangent, normed_three, inverse_three, row(12))
    vg_out[0:1, :] = gain_grad.reshape(1, 512)
    vg_out[1:2, :] = shift_grad.reshape(1, 512)
    grad = back.astype(jnp.bfloat16)
    vg_out[2:3, :] = column_sum(grad).reshape(1, 512)
    incoming = back
    steps = []
    for c in range(chunks):
        span = slice(c * width, c * width + width)
        du = (dot(grad, shrink_ref[span, :], 1, 1) * slopes[:, span]).astype(jnp.bfloat16)
        vg_out[3 + c : 4 + c, :] = column_sum(du).reshape(1, 512)
        incoming = incoming + dot(du, expand_ref[:, span], 1, 1)
        steps.append(du)
    back, gain_grad, shift_grad = norm_backward(incoming, normed_two, inverse_two, row(8))
    back_out[...] = back
    branch = back.astype(jnp.bfloat16)
    branch_out[...] = branch
    do = dot(branch, out_mat_ref[...], 1, 1).astype(jnp.bfloat16)
    for p in range(PLANE):
        dosend[p] = do[:, p * 128 : p * 128 + 128]
    swap_do = Swap(lambda p: dosend.at[p], lambda p: doget.at[p], swap_sems.at[1])
    swap_do.begin()
    vg_out[7:8, :] = gain_grad.reshape(1, 512)
    vg_out[8:9, :] = shift_grad.reshape(1, 512)
    vg_out[9:10, :] = column_sum(branch).reshape(1, 512)
    for c in range(chunks):
        span = slice(c * width, c * width + width)
        grad_shrink[span, :] = dot(actives[:, span], grad, 0, 0).astype(jnp.bfloat16)
        grad_expand[:, span] = dot(low, steps[c], 0, 0).astype(jnp.bfloat16)
    for offset in range(4):
        swap_do.arrived(offset)
    for p in range(PLANE):
        do_out[p * tok : p * tok + tok, :] = doget[p]
    swap.finish()
    swap_do.finish()


def run_centre(wa_count, vec_at, attended, hidden, cotangent, out_mat, expand, shrink, vecs):
    tok = hidden.shape[0]
    low, full = jnp.bfloat16, jnp.float32
    shape = jax.ShapeDtypeStruct
    pairs = pltpu.VMEM((PLANE, tok, 128), low)
    wide = expand.shape[1]
    return pl.pallas_call(
        functools.partial(centre_kernel, wa_count, vec_at),
        out_shape=(shape((tok, 512), full), shape((tok, 512), low), shape((tok, 512), full), shape((tok, 512), low),
                   shape((PLANE * tok, 128), low), shape(shrink.shape, low), shape(expand.shape, low), shape((24, 512), full)),
        in_specs=[VMEM] * 7,
        out_specs=(VMEM,) * 8,
        scratch_shapes=[pairs] * 4 + [pltpu.VMEM((tok, wide), full), pltpu.VMEM((tok, wide), low), DMA((2, 2, 4))],
        compiler_params=pltpu.CompilerParams(collective_id=3, has_side_effects=True, vmem_limit_bytes=60 << 20),
    )(attended, hidden, cotangent, out_mat, expand, shrink, vecs)


def last_kernel(wa_count, shares, at_ref, late_ref, sums_ref, dq_ref, dkv_ref, back_ref, query_mat, key_mat, value_mat,
                expand_ref, shrink_ref, query_out, content_out, expand_out, shrink_out, *outs):
    count = late_ref.shape[1]
    for i in range(count):
        for c in range(PLANE):
            outs[i][:, c * 128 : c * 128 + 128] = late_ref[c, i].astype(jnp.float32)
    query_out[...] = back_ref[...] + dot(dq_ref[...], query_mat[...], 1, 1)
    content_out[...] = dot(dkv_ref[:, :512], key_mat[...], 1, 1) + dot(dkv_ref[:, 512:], value_mat[...], 1, 1)
    expand_out[...] = expand_ref[...].astype(jnp.float32)
    shrink_out[...] = shrink_ref[...].astype(jnp.float32)
    at = 0
    for i, share in enumerate(shares):
        used = share * wa_count // 512
        line = jnp.concatenate([sums_ref[at + r : at + r + 1, :] for r in range(used)], axis=1)
        at += used
        mine = line[:, :share]
        for w in range(1, wa_count):
            mine = jnp.where(at_ref[0] == w, line[:, w * share : w * share + share], mine)
        outs[count + i][...] = mine.reshape(share)


def run_last(wa_count, shares, at, late, sums, dq, dkv, back, query_mat, key_mat, value_mat, expand, shrink):
    full = jnp.float32
    shape = jax.ShapeDtypeStruct
    tok = dq.shape[0]
    out_shape = [shape((tok, 512), full), shape((tok, 512), full), shape(expand.shape, full), shape(shrink.shape, full)]
    out_shape += [shape((late.shape[2], 512), full)] * late.shape[1] + [shape((s,), full) for s in shares]
    return pl.pallas_call(
        functools.partial(last_kernel, wa_count, shares),
        out_shape=tuple(out_shape),
        in_specs=[SMEM] + [VMEM] * 10,
        out_specs=tuple([VMEM] * len(out_shape)),
        compiler_params=pltpu.CompilerParams(vmem_limit_bytes=60 << 20),
    )(at, late, sums, dq, dkv, back, query_mat, key_mat, value_mat, expand, shrink)


def scatter_wide(grad):
    return lax.psum_scatter(grad.astype(jnp.bfloat16), "wa", scatter_dimension=0, tiled=True)


def sum_wide(share):
    return lax.psum(share, ("grp", "pln"))


def shards(
    query_in,
    content_in,
    encoder_in,
    out_grad,
    document_lengths,
    key_ranks,
    query_limits,
    self_query_weight,
    self_query_bias,
    self_key_weight,
    self_value_weight,
    self_value_bias,
    self_out_weight,
    self_out_bias,
    norm_one_gain,
    norm_one_shift,
    cross_query_weight,
    cross_query_bias,
    cross_key_weight,
    cross_value_weight,
    cross_value_bias,
    cross_out_weight,
    cross_out_bias,
    norm_two_gain,
    norm_two_shift,
    expand_weight,
    expand_bias,
    shrink_weight,
    shrink_bias,
    norm_three_gain,
    norm_three_shift,
):
    grp_count = lax.axis_size("grp")
    own = lax.axis_index("grp")[None].astype(jnp.int32)
    lens = document_lengths


    wa_count = lax.axis_size("wa")
    vectors = (self_query_bias, self_value_bias, cross_value_bias, self_out_bias, norm_one_gain, norm_one_shift,
        cross_query_bias, cross_out_bias, norm_two_gain, norm_two_shift, expand_bias, shrink_bias, norm_three_gain,
        norm_three_shift)
    vec_at, at = [], 0
    for v in vectors:
        vec_at.append((at, v.shape[0]))
        at += v.shape[0] // min(128, v.shape[0])
    vec_at = tuple(vec_at)
    mats = (self_key_weight, self_value_weight, self_query_weight, cross_key_weight, cross_value_weight, self_out_weight,
        cross_query_weight, cross_out_weight)
    (self_key_matrix, self_value_mat, self_query_mat, cross_key_matrix, cross_value_mat, self_out_mat, cross_query_mat,
        cross_out_mat, vec_all, pair_one, kv_one, kv_two_own, self_keys, cross_keys, self_marks, cross_marks) = run_opening(
        grp_count, wa_count, lens, key_ranks, query_limits, content_in[0], query_in[0],
        encoder_in[0], vectors, mats, vec_at)
    source = query_in[0]
    content_states = content_in[0]
    encoder_output = encoder_in[0]
    attended_one, total_one = attend_forward(True, lens, own, pair_one, self_marks, kv_one, self_keys)
    hidden_one, normed_one, inverse_one, mixed_one, pair_two, kv_two, expand_mat, shrink_mat = run_middle(
        grp_count, wa_count, attended_one, source, self_out_mat, cross_query_mat, vec_all, vec_at, kv_two_own,
        expand_weight, shrink_weight)
    attended_two, total_two = attend_forward(False, lens, own, pair_two, cross_marks, kv_two, cross_keys)
    layer_out, mixed_two, back_two, branch_two, do_two, grad_shrink_mat, grad_expand_mat, lines = run_centre(
        wa_count, vec_at, attended_two, hidden_one, out_grad[0], cross_out_mat, expand_mat, shrink_mat, vec_all)
    grad_shrink_mat = scatter_wide(grad_shrink_mat)
    grad_expand_mat = scatter_wide(grad_expand_mat)
    dq_two, dkv_two, own_two = attend_backward(False, lens, own, pair_two, cross_marks, kv_two, cross_keys,
        attended_two, total_two, do_two)
    do_one, back_one, kv_two_grad, early, lines = run_turn(grp_count, wa_count, vec_at, dq_two, dkv_two, own_two, back_two,
        normed_one, inverse_one, hidden_one, mixed_one, mixed_two, branch_two, encoder_output, cross_query_mat, self_out_mat,
        vec_all, lines)
    do_one, grad_shrink_mat, grad_expand_mat = lax.optimization_barrier((do_one, grad_shrink_mat, grad_expand_mat))
    grad_shrink_mat = sum_wide(grad_shrink_mat)
    grad_expand_mat = sum_wide(grad_expand_mat)
    key_two_low, value_two_low = kv_two_grad[:, :512], kv_two_grad[:, 512:]
    encoder_grad = right_product(key_two_low, cross_key_matrix) + right_product(value_two_low, cross_value_mat)
    dq_one, dkv_one, own_one = attend_backward(True, lens, own, pair_one, self_marks, kv_one, self_keys,
        attended_one, total_one, do_one)
    query_one_low, kv_one_grad, late, sums = run_closing(grp_count, wa_count, dq_one, dkv_one, own_one, source,
        content_states, early, lines)
    shares = tuple(v.shape[0] for v in (norm_three_gain, norm_three_shift, shrink_bias, expand_bias, norm_two_gain,
        norm_two_shift, cross_out_bias, norm_one_gain, norm_one_shift, self_out_bias, cross_query_bias, cross_value_bias,
        self_query_bias, self_value_bias))
    query_grad, content_grad, expand_grad, shrink_grad, *rest = run_last(wa_count, shares,
        lax.axis_index("wa")[None].astype(jnp.int32), late, sums, query_one_low, kv_one_grad, back_one, self_query_mat,
        self_key_matrix, self_value_mat, grad_expand_mat, grad_shrink_mat)
    names = ("cross_out", "cross_query", "self_out", "cross_key", "cross_value", "self_query", "self_key", "self_value")
    mat = dict(zip(names, rest))
    names = ("gain_three", "shift_three", "shrink", "expand", "gain_two", "shift_two", "cross_out", "gain_one", "shift_one",
        "self_out", "cross_query", "cross_value", "self_query", "self_value")
    vec = dict(zip(names, rest[len(mat):]))
    grads = (mat["self_query"], vec["self_query"], mat["self_key"], mat["self_value"], vec["self_value"], mat["self_out"],
        vec["self_out"], vec["gain_one"], vec["shift_one"], mat["cross_query"], vec["cross_query"], mat["cross_key"],
        mat["cross_value"], vec["cross_value"], mat["cross_out"], vec["cross_out"], vec["gain_two"], vec["shift_two"],
        expand_grad, vec["expand"], shrink_grad, vec["shrink"], vec["gain_three"], vec["shift_three"])
    return (layer_out[None], query_grad[None], content_grad[None], encoder_grad[None]) + grads


def solution(mesh):
    ctx, wa = mesh.devices.shape
    mesh = Mesh(mesh.devices.reshape(ctx // PLANE, PLANE, wa), ("grp", "pln", "wa"))
    in_specs = (
        P("wa", ("grp", "pln"), None),
        P("wa", ("grp", "pln"), None),
        P("wa", ("grp", "pln"), None),
        P("wa", ("grp", "pln"), None),
        P("wa", None),
        P("wa", None),
        P("wa", None),
        P("wa", None),
        P("wa"),
        P("wa", None),
        P("wa", None),
        P("wa"),
        P("wa", None),
        P("wa"),
        P("wa"),
        P("wa"),
        P("wa", None),
        P("wa"),
        P("wa", None),
        P("wa", None),
        P("wa"),
        P("wa", None),
        P("wa"),
        P("wa"),
        P("wa"),
        P("wa", None),
        P("wa"),
        P("wa", None),
        P("wa"),
        P("wa"),
        P("wa"),
    )
    out_specs = (
        P("wa", ("grp", "pln"), None),
        P("wa", ("grp", "pln"), None),
        P("wa", ("grp", "pln"), None),
        P("wa", ("grp", "pln"), None),
        P("wa", None),
        P("wa"),
        P("wa", None),
        P("wa", None),
        P("wa"),
        P("wa", None),
        P("wa"),
        P("wa"),
        P("wa"),
        P("wa", None),
        P("wa"),
        P("wa", None),
        P("wa", None),
        P("wa"),
        P("wa", None),
        P("wa"),
        P("wa"),
        P("wa"),
        P("wa", None),
        P("wa"),
        P("wa", None),
        P("wa"),
        P("wa"),
        P("wa"),
    )
    return jax.shard_map(shards, mesh=mesh, in_specs=in_specs, out_specs=out_specs, check_vma=False)
```

profile of v0, /device:TPU:0, one launch (start us, length us, event | category | flops | bytes accessed | tf_op | source)
XLA Modules:
  0.0 351.8 jit_solution(1641444872857057418)
XLA Ops:
  7.2 0.0 reduce-scatter.3.cloned.1.call-start
  7.3 45.6 %shard_map.510 = (bf16[512,512]{1,0:T(8,128)(2,1)}, bf16[512,512]{1,0:T(8,128)(2,1)}, bf16[512,512]{1,0:T(8,128)(2,1)}, bf16[512,512]{1,0:T(8,128)(2,1)}, bf16[5...) custom-call(s32[1,4]{1,0:T(1,128)} %lens_ref.9, ...), custom_call_target="tpu_custom_call" | custom-call | flops 38000001024 | tf_op jit(solution)/shard_map/pallas_call | solution.py:636
  52.9 13.4 %shard_map.511 = (f32[1024,128]{1,0:T(8,128)}, f32[1024,128]{1,0:T(8,128)}) custom-call(s32[1,4]{1,0:T(1,128)} %lens_ref.9, s32[1]{0:T(128)} %bitcast.own_ref, bf16[1024,128]{1,0:T(8,128)(2,1)} %get-tuple-element.108.q_ref, bf16[1024,128]{1,0:T(8,128)(2,1)} %get-tuple-element.109.qm_ref, bf16[4096,256]{1,0:T(8,128)(2,1)} %get-tuple-element.110.kv_ref, ...), custom_call_target="tpu_custom_call" | custom-call | flops 12000000000 | tf_op jit(solution)/shard_map/pallas_call | solution.py:116
  66.2 31.8 %shard_map.512 = (f32[256,512]{1,0:T(8,128)}, f32[256,512]{1,0:T(8,128)}, f32[256,128]{1,0:T(8,128)}, bf16[256,512]{1,0:T(8,128)(2,1)}, bf16[1024,128]{1,0:T(8,1...) custom-call(f32[1024,128]{1,0:T(8,128)} %get-tuple-element.112.attended_ref.o_ref, ...), custom_call_target="tpu_custom_call" | custom-call | flops 30000001024 | tf_op jit(solution)/shard_map/pallas_call | solution.py:720
  98.0 13.9 %shard_map.513 = (f32[1024,128]{1,0:T(8,128)}, f32[1024,128]{1,0:T(8,128)}) custom-call(s32[1,4]{1,0:T(1,128)} %lens_ref.9, s32[1]{0:T(128)} %bitcast.own_ref, bf16[1024,128]{1,0:T(8,128)(2,1)} %get-tuple-element.117.q_ref, bf16[1024,128]{1,0:T(8,128)(2,1)} %get-tuple-element.118.qm_ref, bf16[4096,256]{1,0:T(8,128)(2,1)} %get-tuple-element.119.kv_ref, ...), custom_call_target="tpu_custom_call" | custom-call | flops 12000000000 | tf_op jit(solution)/shard_map/pallas_call | solution.py:116
  111.9 20.7 %shard_map.514 = (f32[256,512]{1,0:T(8,128)}, bf16[256,512]{1,0:T(8,128)(2,1)}, f32[256,512]{1,0:T(8,128)}, bf16[256,512]{1,0:T(8,128)(2,1)}, bf16[1024,128]{1,0...) custom-call(f32[1024,128]{1,0:T(8,128)} %get-tuple-element.121.attended_ref.o_ref, ...), custom_call_target="tpu_custom_call" | custom-call | tf_op jit(solution)/shard_map/pallas_call | solution.py:1341
  132.6 0.0 reduce-scatter.3.cloned.1.call-update
  132.6 0.0 reduce-scatter.5.cloned.1.call-start
  132.7 0.7 reduce-scatter.5.cloned.1.call-update
  133.4 0.0 all-reduce.3.cloned.1.call-start
  133.4 28.7 %shard_map.515 = (bf16[1024,128]{1,0:T(8,128)(2,1)}, bf16[4096,256]{1,0:T(8,128)(2,1)}, f32[1024,256]{1,0:T(8,128)}) custom-call(s32[1,4]{1,0:T(1,128)} %lens_ref.9, s32[1]{0:T(128)} %bitcast.own_ref, bf16[1024,128]{1,0:T(8,128)(2,1)} %get-tuple-element.117.q_ref, bf16[1024,128]{1,0:T(8,128)(2,1)} %get-tuple-element.118.qm_ref, ...), custom_call_target="tpu_custom_call" | custom-call | flops 25999998976 | tf_op jit(solution)/shard_map/pallas_call | solution.py:211
  162.1 0.0 copy-start.2
  162.1 0.0 copy-start
  162.1 33.2 %shard_map.516 = (bf16[1024,128]{1,0:T(8,128)(2,1)}, f32[256,512]{1,0:T(8,128)}, bf16[256,1024]{1,0:T(8,128)(2,1)}, bf16[5,4,512,128]{3,2,1,0:T(8,128)(2,1)}, f32[24,512]{1,0:T(8,128)}) custom-call(bf16[1024,128]{1,0:T(8,128)(2,1)} %get-tuple-element.130.dq_ref, bf16[4096,256]{1,0:T(8,128)(2,1)} %get-tuple-element.131.dkv_ref, ...), custom_call_target="tpu_custom_call" | custom-call | flops 32000000000 | tf_op jit(solution)/shard_map/pallas_call | solution.py:951
  195.3 0.0 copy-done.2
  195.3 1.3 fusion.2
  196.6 0.0 copy-done
  196.6 2.1 fusion
  198.7 0.0 reduce-scatter.3.cloned.1.call-done
  198.7 0.0 reduce-scatter.5.cloned.1.call-done
  198.7 28.6 %shard_map.517 = (bf16[1024,128]{1,0:T(8,128)(2,1)}, bf16[4096,256]{1,0:T(8,128)(2,1)}, f32[1024,256]{1,0:T(8,128)}) custom-call(s32[1,4]{1,0:T(1,128)} %lens_ref.9, s32[1]{0:T(128)} %bitcast.own_ref, bf16[1024,128]{1,0:T(8,128)(2,1)} %get-tuple-element.108.q_ref, bf16[1024,128]{1,0:T(8,128)(2,1)} %get-tuple-element.109.qm_ref, ...), custom_call_target="tpu_custom_call" | custom-call | flops 25999998976 | tf_op jit(solution)/shard_map/pallas_call | solution.py:211
  227.4 0.0 all-reduce.3.cloned.1.call-update
  227.4 95.4 %shard_map.518 = (bf16[256,512]{1,0:T(8,128)(2,1)}, bf16[256,1024]{1,0:T(8,128)(2,1)}, bf16[4,8,256,128]{3,2,1,0:T(8,128)(2,1)}, f32[24,512]{1,0:T(8,128)}) custom-call(bf16[1024,128]{1,0:T(8,128)(2,1)} %get-tuple-element.144.dq_ref, bf16[4096,256]{1,0:T(8,128)(2,1)} %get-tuple-element.145.dkv_ref, f32[1024,256]{1,0:T(8,128)} %get-tuple-element.146.own_ref, ...), custom_call_target="tpu_custom_call" | custom-call | flops 74999996416 | tf_op jit(solution)/shard_map/pallas_call | solution.py:1245
  322.9 14.2 %all-reduce.3.cloned.1.call-done = (bf16[256,2048]{1,0:T(8,128)(2,1)}, bf16[1024,512]{1,0:T(8,128)(2,1)}) async-done(((bf16[256,2048]{1,0:T(8,128)(2,1)}, bf16[1024,512]{1,0:T(8,128)(2,1)}), (bf16[256,2048]{1,0:T(8,128)(2,1)}, bf16[1024,512]{1,0:T(8,128)(2,1)})) %all-reduce.3.cloned.1.call-update) | async-done | bytes 2097168 | tf_op jit(solution)/shard_map/psum | solution.py:1393
  337.1 0.0 copy-start.1
  337.1 7.4 %shard_map.519 = (f32[256,512]{1,0:T(8,128)}, f32[256,512]{1,0:T(8,128)}, f32[256,2048]{1,0:T(8,128)}, f32[1024,512]{1,0:T(8,128)}, f32[256,512]{1,0:T(8,128)}, ...) custom-call(s32[1]{0:T(128)} %bitcast.6.at_ref, ...), custom_call_target="tpu_custom_call" | custom-call | tf_op jit(solution)/shard_map/pallas_call | solution.py:1379
  344.5 0.0 copy-done.1
  344.5 0.8 copy.62
Async XLA Ops:
  7.2 191.5 %reduce-scatter.3.cloned.1.call-start = ((), (), s32[]{:S(2)}) async-start(), calls=%async_computation.2 | async-start | bytes 3145728 | tf_op jit(solution)/shard_map/reduce_scatter | solution.py:1389
  132.6 66.1 %reduce-scatter.5.cloned.1.call-start = ((), (), s32[]{:S(2)}) async-start(), calls=%async_computation.3 | async-start | bytes 3145728 | tf_op jit(solution)/shard_map/reduce_scatter | solution.py:1389
  133.4 203.7 %all-reduce.3.cloned.1.call-start = ((), (), s32[]{:S(2)}) async-start(), calls=%async_computation.4 | async-start | bytes 4194304 | tf_op jit(solution)/shard_map/psum | solution.py:1393
  162.1 33.2 %copy-start.2 = (bf16[512,512]{1,0:T(8,128)(2,1)S(1)}, bf16[512,512]{1,0:T(8,128)(2,1)}, u32[]{:S(2)}) copy-start(bf16[512,512]{1,0:T(8,128)(2,1)} %get-tuple-element.162) | copy-start | bytes 1572868
  162.1 34.5 %copy-start = (bf16[512,512]{1,0:T(8,128)(2,1)S(1)}, bf16[512,512]{1,0:T(8,128)(2,1)}, u32[]{:S(2)}) copy-start(bf16[512,512]{1,0:T(8,128)(2,1)} %get-tuple-element.163) | copy-start | bytes 1572868
  337.1 7.4 %copy-start.1 = (f32[256,512]{1,0:T(8,128)S(1)}, f32[256,512]{1,0:T(8,128)}, u32[]{:S(2)}) copy-start(f32[256,512]{1,0:T(8,128)} %get-tuple-element.126) | copy-start | bytes 1572868
Sparse Core Ops, SparseCore 0:
  132.7 29.0 reduce-scatter.2
  164.2 31.8 reduce-scatter.4
  227.5 109.4 all-reduce.2
where the time goes:
time: 357 us; the launch traced here: 352 us
  Pallas kernels  319 us (89%)
  waiting for transfers between devices  14.9 us (4%)
  between operations  13.9 us (4%)
    pallas_call x1, Pallas kernels, run_closing(): pl.pallas_call(functools.partial(closing_kernel, grp_count, wa_count, rea...  95.4 us
    pallas_call x2, Pallas kernels, attend_backward(): pl.pallas_call(functools.partial(backward_kernel, ranked), out_shape=(jax...  57.3 us
    pallas_call x1, Pallas kernels, run_opening(): pl.pallas_call(functools.partial(opening_kernel, grp_count, wa_count, rea...  45.6 us
    pallas_call x1, Pallas kernels, run_turn(): pl.pallas_call(functools.partial(turn_kernel, grp_count, wa_count, reach,...  33.2 us
    pallas_call x1, Pallas kernels, run_middle(): pl.pallas_call(functools.partial(middle_kernel, grp_count, wa_count, reac...  31.8 us
    pallas_call x2, Pallas kernels, attend_forward(): pl.pallas_call(functools.partial(forward_kernel, ranked), out_shape=(jax....  27.2 us
    pallas_call x1, Pallas kernels, run_centre(): pl.pallas_call(functools.partial(centre_kernel, wa_count, vec_at), out_sh...  20.7 us
    psum x1, waiting for transfers between devices, sum_wide(): return lax.psum(share, ('grp', 'pln'))  14.2 us
  transfers between devices with their start and end apart: 3, of which 1 were waited for; matrix products, arithmetic and copies ran while one was open for 1% of the time, Pallas kernels for 45%

commit v1 on v0

--- a/solution.py
+++ b/solution.py
@@ -14,8 +14,10 @@
 INV_ROOT_TWO_PI = 0.3989422804014327
 NEGATIVE = -1e29
 HIDE = -(2.0 ** 100)
-BLOCK = 256
-WIDE = 512
+BLOCK = 512
+WIDE = 1024
+QUERIES = 512
+KEYS = 512
 STAT = 40
 
 
@@ -61,19 +63,29 @@
     return carry
 
 
+def turned(value, eye):
+    return dot(eye, value, 1, 1).astype(jnp.bfloat16)
+
+
+def unit_matrix():
+    row = lax.broadcasted_iota(jnp.int32, (128, 128), 0)
+    lane = lax.broadcasted_iota(jnp.int32, (128, 128), 1)
+    return jnp.where(row == lane, 1.0, 0.0).astype(jnp.bfloat16)
+
+
 def forward_kernel(ranked, lens_ref, own_ref, q_ref, qm_ref, kv_ref, km_ref, o_ref, lse_ref):
     rows = q_ref.shape[0]
     base = own_ref[0] * rows
-    half = left_half((BLOCK, 128))
+    half = left_half((QUERIES, 128))
     khalf = left_half((WIDE, 128))
     one = jnp.ones((WIDE, 128), jnp.bfloat16)
 
     def one_block(block, _):
-        start = pl.multiple_of(block * BLOCK, BLOCK)
+        start = pl.multiple_of(block * QUERIES, QUERIES)
         first = base + start
-        low, high = spans(lens_ref, first, BLOCK)
-        q = q_ref[pl.ds(start, BLOCK), :]
-        qm = qm_ref[pl.ds(start, BLOCK), :]
+        low, high = spans(lens_ref, first, QUERIES)
+        q = q_ref[pl.ds(start, QUERIES), :]
+        qm = qm_ref[pl.ds(start, QUERIES), :]
         queries = (jnp.where(half, q, qm), jnp.where(half, qm, q))
 
         def step(at, carry, diagonal=False):
@@ -84,9 +96,9 @@
             values = (jnp.where(khalf, v, one), jnp.where(khalf, one, v))
             scores = [dot(queries[h], keys[h], 1, 1) for h in (0, 1)]
             if diagonal:
-                place = first + lax.broadcasted_iota(jnp.int32, (BLOCK, WIDE), 0)
-                other = at + lax.broadcasted_iota(jnp.int32, (BLOCK, WIDE), 1)
-                column = first + lax.broadcasted_iota(jnp.int32, (BLOCK, 1), 0)
+                place = first + lax.broadcasted_iota(jnp.int32, (QUERIES, WIDE), 0)
+                other = at + lax.broadcasted_iota(jnp.int32, (QUERIES, WIDE), 1)
+                column = first + lax.broadcasted_iota(jnp.int32, (QUERIES, 1), 0)
                 banned = jnp.where(openings(lens_ref, column), -1, place) == other
                 scores = [jnp.where(banned, HIDE, s) for s in scores]
             out = []
@@ -98,15 +110,15 @@
                 out.append((new, acc))
             return tuple(out)
 
-        empty = (jnp.full((BLOCK, 1), NEGATIVE, jnp.float32), jnp.zeros((BLOCK, 128), jnp.float32))
+        empty = (jnp.full((QUERIES, 1), NEGATIVE, jnp.float32), jnp.zeros((QUERIES, 128), jnp.float32))
         (peak0, acc0), (peak1, acc1) = over_blocks(low, high, first, WIDE, step, (empty, empty), ranked)
         total = jnp.where(half, acc1, acc0)
         mixed = jnp.where(half, acc0, acc1)
-        o_ref[pl.ds(start, BLOCK), :] = mixed / pltpu.roll(total, 64, 1)
-        lse_ref[pl.ds(start, BLOCK), :] = jnp.where(half, peak1, peak0) + jnp.log(total)
+        o_ref[pl.ds(start, QUERIES), :] = mixed / pltpu.roll(total, 64, 1)
+        lse_ref[pl.ds(start, QUERIES), :] = jnp.where(half, peak1, peak0) + jnp.log(total)
         return 0
 
-    lax.fori_loop(0, rows // BLOCK, one_block, 0)
+    lax.fori_loop(0, rows // QUERIES, one_block, 0)
 
 
 def attend_forward(ranked, lens, own, q, qm, kv, km):
@@ -133,12 +145,13 @@
 
 
 def backward_kernel(ranked, lens_ref, own_ref, q_ref, qm_ref, kv_ref, km_ref, o_ref, lse_ref, do_ref,
-                    dq_ref, dkv_ref, own_dkv_ref, dk_ref, dv_ref):
+                    dq_ref, dkv_ref, own_dkv_ref, dk_ref, dv_ref, kt0_ref, kt1_ref):
     rows = q_ref.shape[0]
     base = own_ref[0] * rows
     half = left_half((BLOCK, 128))
+    khalf = left_half((KEYS, 128))
     lane = lax.broadcasted_iota(jnp.int32, (BLOCK, 128), 1)
-    one = jnp.ones((BLOCK, 128), jnp.bfloat16)
+    one = jnp.ones((KEYS, 128), jnp.bfloat16)
     zero = jnp.zeros((BLOCK, 128), jnp.bfloat16)
 
     def clear(index, _):
@@ -148,6 +161,19 @@
         return 0
 
     lax.fori_loop(0, kv_ref.shape[0] // BLOCK, clear, 0)
+    eye = unit_matrix()
+    tops = lax.broadcasted_iota(jnp.int32, (128, KEYS), 0) < 64
+    low_all, high_all = spans(lens_ref, base, rows)
+
+    def prepare(block, _):
+        there = pl.ds(pl.multiple_of(block * KEYS, KEYS), KEYS)
+        kt = turned(kv_ref[there, :128], eye)
+        none = jnp.zeros((128, KEYS), jnp.bfloat16)
+        kt0_ref[:, there] = jnp.where(tops, kt, none)
+        kt1_ref[:, there] = jnp.where(tops, none, kt)
+        return 0
+
+    lax.fori_loop(low_all // KEYS, (high_all + KEYS - 1) // KEYS, prepare, 0)
 
     def one_block(block, _):
         start = pl.multiple_of(block * BLOCK, BLOCK)
@@ -163,31 +189,29 @@
         side = with_stat(zero, -jnp.where(half, delta1, delta0), lane % 64, STAT)
         grads = (jnp.where(half, do, side), jnp.where(half, side, do))
 
+        both_q = jnp.concatenate([jnp.where(half, q, zero), jnp.where(half, zero, q)], axis=0)
+        both_do = jnp.concatenate([jnp.where(half, do, zero), jnp.where(half, zero, do)], axis=0)
+
         def step(at, carry, diagonal=False):
-            there = pl.ds(at, BLOCK)
+            there = pl.ds(at, KEYS)
             k, v, km = kv_ref[there, :128], kv_ref[there, 128:], km_ref[there, :]
-            keys = (jnp.where(half, k, km), jnp.where(half, km, k))
-            values = (jnp.where(half, v, one), jnp.where(half, one, v))
+            keys = (jnp.where(khalf, k, km), jnp.where(khalf, km, k))
+            values = (jnp.where(khalf, v, one), jnp.where(khalf, one, v))
             scores = [dot(keys[h], queries[h], 1, 1) for h in (0, 1)]
             if diagonal:
-                other = first + lax.broadcasted_iota(jnp.int32, (BLOCK, BLOCK), 0)
+                other = at + lax.broadcasted_iota(jnp.int32, (KEYS, BLOCK), 0)
                 row = first + lax.broadcasted_iota(jnp.int32, (1, BLOCK), 1)
                 banned = other == jnp.where(openings(lens_ref, row), -1, row)
                 scores = [jnp.where(banned, HIDE, s) for s in scores]
-            dvs, dks, dqs = [], [], []
-            for h in (0, 1):
-                p = jnp.exp(scores[h])
-                dp = dot(values[h], grads[h], 1, 1)
-                ds = (p * dp).astype(jnp.bfloat16)
-                dvs.append(dot(p.astype(jnp.bfloat16), do, 1, 0))
-                dks.append(dot(ds, q, 1, 0))
-                dqs.append(dot(ds, k, 0, 0))
-            dv_ref[there, :] += jnp.where(half, dvs[0], dvs[1])
-            dk_ref[there, :] += jnp.where(half, dks[0], dks[1])
-            return carry + jnp.where(half, dqs[0], dqs[1])
-
-        dq = over_blocks(low, high, first, BLOCK, step, jnp.zeros((BLOCK, 128), jnp.float32), ranked)
-        dq_ref[here, :] = (dq * 0.125).astype(dq_ref.dtype)
+            ps = [jnp.exp(scores[h]) for h in (0, 1)]
+            ds = [(ps[h] * dot(values[h], grads[h], 1, 1)).astype(jnp.bfloat16) for h in (0, 1)]
+            ps = [p.astype(jnp.bfloat16) for p in ps]
+            dv_ref[there, :] += dot(jnp.concatenate(ps, axis=1), both_do, 1, 0)
+            dk_ref[there, :] += dot(jnp.concatenate(ds, axis=1), both_q, 1, 0)
+            return carry + dot(kt0_ref[:, there], ds[0], 1, 0) + dot(kt1_ref[:, there], ds[1], 1, 0)
+
+        dq = over_blocks(low, high, first, KEYS, step, jnp.zeros((128, BLOCK), jnp.float32), ranked)
+        dq_ref[here, :] = jnp.transpose(dq * 0.125).astype(dq_ref.dtype)
         return 0
 
     lax.fori_loop(0, rows // BLOCK, one_block, 0)
@@ -214,7 +238,7 @@
             jax.ShapeDtypeStruct((keys, 256), jnp.bfloat16), jax.ShapeDtypeStruct((rows, 256), jnp.float32)),
         in_specs=[smem, smem] + [whole] * 7,
         out_specs=(whole, whole, whole),
-        scratch_shapes=[pltpu.VMEM((keys, 128), jnp.float32)] * 2,
+        scratch_shapes=[pltpu.VMEM((keys, 128), jnp.float32)] * 2 + [pltpu.VMEM((128, keys), jnp.bfloat16)] * 2,
         cost_estimate=pl.CostEstimate(flops=26000000000, bytes_accessed=0, transcendentals=0),
         compiler_params=pltpu.CompilerParams(vmem_limit_bytes=60 << 20),
     )(lens, own, q, qm, kv, km, o, lse, do)
@@ -867,25 +891,101 @@
     return keys, values
 
 
+class Reduce:
+    def __init__(self, index, source, parts, got, kept, sems, wa_count, place=None):
+        self.index, self.source, self.sems, self.wa_count = index, source, sems, wa_count
+        self.parts, (self.got_core, self.got_wa, self.got_row) = parts, got
+        self.by_core, self.by_wa, self.by_row = kept
+        self.place = index if place is None else place
+        self.wa, self.pln = lax.axis_index("wa"), lax.axis_index("pln")
+        self.core = lax.rem(self.pln, 2)
+        self.row = self.pln // 2
+        self.size = 512 // wa_count
+
+    def core_copy(self, row):
+        return remote(self.source.at[row * 2 + 1 - self.core], self.got_core.at[self.index, row],
+                      self.sems.at[0, self.index, row], self.sems.at[1, self.index, row], {"pln": across(self.pln, 1)})
+
+    def rows_of(self, wa):
+        return pl.ds(pl.multiple_of(wa * self.size, 16), self.size)
+
+    def wa_copy(self, offset):
+        peer = lax.rem(self.wa + offset, self.wa_count)
+        return remote(self.by_core.at[self.index, :, self.rows_of(peer)], self.got_wa.at[offset - 1, self.index],
+                      self.sems.at[0, self.index, 1 + offset], self.sems.at[1, self.index, 1 + offset], {"wa": peer})
+
+    def row_copy(self):
+        return remote(self.by_wa.at[self.index, 1 - self.row], self.got_row.at[self.index],
+                      self.sems.at[0, self.index, 1 + self.wa_count], self.sems.at[1, self.index, 1 + self.wa_count],
+                      {"pln": across(self.pln, 2)})
+
+    def begin(self):
+        for row in (0, 1):
+            self.core_copy(row).start()
+
+    def after_core(self):
+        for row in (0, 1):
+            self.core_copy(row).wait_recv()
+            mine = self.parts[row * 2 + self.core].astype(jnp.float32)
+            total = mine + self.got_core[self.index, row].astype(jnp.float32)
+            self.by_core[self.index, row] = total.astype(jnp.bfloat16)
+        for offset in range(1, self.wa_count):
+            self.wa_copy(offset).start()
+
+    def after_wa(self):
+        for offset in range(1, self.wa_count):
+            self.wa_copy(offset).wait_recv()
+        for row in (0, 1):
+            total = self.by_core[self.index, row, self.rows_of(self.wa), :].astype(jnp.float32)
+            for offset in range(1, self.wa_count):
+                total = total + self.got_wa[offset - 1, self.index, row].astype(jnp.float32)
+            self.by_wa[self.index, row] = total.astype(jnp.bfloat16)
+        self.row_copy().start()
+
+    def after_row(self):
+        self.row_copy().wait_recv()
+        total = self.by_wa[self.index, self.row].astype(jnp.float32) + self.got_row[self.index].astype(jnp.float32)
+        self.by_row[self.place] = total.astype(jnp.bfloat16)
+
+    def finish(self):
+        for row in (0, 1):
+            self.core_copy(row).wait_send()
+        for offset in range(1, self.wa_count):
+            self.wa_copy(offset).wait_send()
+        self.row_copy().wait_send()
+
+
 def turn_kernel(grp_count, wa_count, reach, vec_at, dq_ref, dkv_ref, own_ref, back_ref, normed_ref, inverse_ref, hidden_ref,
-                mixed_one_ref, mixed_two_ref, branch_two_ref, encoder_ref, query_mat_ref, out_mat_ref, vec_ref, vg_ref,
-                do_out, back_out, kv_out, grads_out, vg_out,
-                dqsend, dqget, dosend, doget, kvsend, kvget, total, mine, foldsend, foldget, grads, fold_sems, load_sems,
-                swap_sems, out_sems):
+                mixed_one_ref, mixed_two_ref, branch_two_ref, encoder_ref, query_mat_ref, out_mat_ref, vec_ref, vg_ref, wide_ref,
+                do_out, back_out, kv_out, grads_out, vg_out, wide_out,
+                dqsend, dqget, dosend, doget, kvsend, kvget, total, mine, foldsend, foldget, grads, parts, got_core, got_wa,
+                got_row, by_core, by_wa, by_row, fold_sems, load_sems, swap_sems, out_sems, part_sems, red_sems):
     tok = back_ref.shape[0]
     for p in range(PLANE):
         dqsend[p] = dq_ref[p * tok : p * tok + tok, :]
-    greet(grp_count, wa_count, rows=False)
+    wide = wide_ref.shape[0]
+    loads = [pltpu.make_async_copy(wide_ref.at[i], parts.at[i], part_sems.at[i]) for i in range(wide)]
+    for l in loads:
+        l.start()
+    greet(grp_count, wa_count)
     swap_dq = Swap(lambda p: dqsend.at[p], lambda p: dqget.at[p], swap_sems.at[0])
     swap_dq.begin()
     fold = Fold(dkv_ref, mine, foldsend, foldget, fold_sems, load_sems, grp_count, reach, tok)
     fold.begin()
+    reds = [Reduce(i, wide_ref.at[i], parts.at[i], (got_core, got_wa, got_row), (by_core, by_wa, by_row), red_sems, wa_count)
+            for i in range(wide)]
+    for r in reds:
+        r.begin()
     row = lambda i: vector_row(vec_ref, wa_count, *vec_at[i])
     vg_out[...] = vg_ref[...]
     saves = [pltpu.make_async_copy(grads.at[i], grads_out.at[i], out_sems.at[i]) for i in range(5)]
     total[...] = own_ref[...]
     store_blocks(grads.at[0], dot(mixed_two_ref[...], branch_two_ref[...], 0, 0))
     saves[0].start()
+    for l in loads:
+        l.wait()
+    for r in reds:
+        r.after_core()
     for offset in range(4):
         swap_dq.arrived(offset)
     dq = flat_pairs(dqget)
@@ -912,6 +1012,8 @@
         swap_do.arrived(offset)
     for p in range(PLANE):
         do_out[p * tok : p * tok + tok, :] = doget[p]
+    for r in reds:
+        r.after_wa()
     fold.total(total, kvsend)
     swap_kv = Swap(lambda p: kvsend.at[p], lambda p: kvget.at[p], swap_sems.at[2])
     swap_kv.begin()
@@ -926,8 +1028,15 @@
     store_blocks(grads.at[4], dot(encoder, values, 0, 0))
     saves[4].start()
     vg_out[14:15, :] = column_sum(values).reshape(1, 512)
+    for r in reds:
+        r.after_row()
+    wide_save = pltpu.make_async_copy(by_row, wide_out, part_sems.at[0])
+    wide_save.start()
     for s in saves:
         s.wait()
+    for r in reds:
+        r.finish()
+    wide_save.wait()
     fold.finish()
     for s in (swap_dq, swap_do, swap_kv):
         s.finish()
@@ -942,87 +1051,29 @@
 
 
 def run_turn(grp_count, wa_count, vec_at, dq, dkv, own, back, normed, inverse, hidden, mixed_one, mixed_two, branch_two,
-             encoder, query_mat, out_mat, vecs, vg):
+             encoder, query_mat, out_mat, vecs, vg, wide):
     tok = back.shape[0]
     reach = min(grp_count - 1, (DOCLEN + PLANE * tok - 2) // (PLANE * tok))
     low, full = jnp.bfloat16, jnp.float32
     shape = jax.ShapeDtypeStruct
     pairs = pltpu.VMEM((PLANE, tok, 128), low)
+    count, size = wide.shape[0], 512 // wa_count
     return pl.pallas_call(
         functools.partial(turn_kernel, grp_count, wa_count, reach, vec_at),
         out_shape=(shape((PLANE * tok, 128), low), shape((tok, 512), full), shape((tok, 1024), low),
-                   shape((5, PLANE, 512, 128), low), shape(vg.shape, full)),
-        in_specs=[VMEM, ANY] + [VMEM] * 13,
-        out_specs=(VMEM, VMEM, VMEM, ANY, VMEM),
+                   shape((5, PLANE, 512, 128), low), shape(vg.shape, full), shape((count, size, 128), low)),
+        in_specs=[VMEM, ANY] + [VMEM] * 13 + [ANY],
+        out_specs=(VMEM, VMEM, VMEM, ANY, VMEM, ANY),
         scratch_shapes=[pairs] * 4 + fold_scratch(tok, reach) + [
-            pltpu.VMEM((5, PLANE, 512, 128), low), DMA((2, 2, reach, PLANE)), DMA((2, max(1, reach - 1))), DMA((3, 2, 4)),
-            DMA((5,))],
+            pltpu.VMEM((5, PLANE, 512, 128), low), pltpu.VMEM((count, PLANE, 512, 128), low),
+            pltpu.VMEM((count, 2, 512, 128), low), pltpu.VMEM((max(1, wa_count - 1), count, 2, size, 128), low),
+            pltpu.VMEM((count, size, 128), low), pltpu.VMEM((count, 2, 512, 128), low), pltpu.VMEM((count, 2, size, 128), low),
+            pltpu.VMEM((count, size, 128), low), DMA((2, 2, reach, PLANE)), DMA((2, max(1, reach - 1))), DMA((3, 2, 4)),
+            DMA((5,)), DMA((count,)), DMA((2, count, wa_count + 2))],
         cost_estimate=pl.CostEstimate(flops=32000000000, bytes_accessed=0, transcendentals=0),
         compiler_params=pltpu.CompilerParams(collective_id=8, has_side_effects=True, vmem_limit_bytes=60 << 20),
-    )(dq, dkv, own, back, normed, inverse, hidden, mixed_one, mixed_two, branch_two, encoder, query_mat, out_mat, vecs, vg)
-
-
-class Reduce:
-    def __init__(self, index, source, parts, got, kept, sems, wa_count):
-        self.index, self.source, self.sems, self.wa_count = index, source, sems, wa_count
-        self.parts, (self.got_core, self.got_wa, self.got_row) = parts, got
-        self.by_core, self.by_wa, self.by_row = kept
-        self.wa, self.pln = lax.axis_index("wa"), lax.axis_index("pln")
-        self.core = lax.rem(self.pln, 2)
-        self.row = self.pln // 2
-        self.size = 512 // wa_count
-
-    def core_copy(self, row):
-        return remote(self.source.at[row * 2 + 1 - self.core], self.got_core.at[self.index, row],
-                      self.sems.at[0, self.index, row], self.sems.at[1, self.index, row], {"pln": across(self.pln, 1)})
-
-    def rows_of(self, wa):
-        return pl.ds(pl.multiple_of(wa * self.size, 16), self.size)
-
-    def wa_copy(self, offset):
-        peer = lax.rem(self.wa + offset, self.wa_count)
-        return remote(self.by_core.at[self.index, :, self.rows_of(peer)], self.got_wa.at[offset - 1, self.index],
-                      self.sems.at[0, self.index, 1 + offset], self.sems.at[1, self.index, 1 + offset], {"wa": peer})
-
-    def row_copy(self):
-        return remote(self.by_wa.at[self.index, 1 - self.row], self.got_row.at[self.index],
-                      self.sems.at[0, self.index, 1 + self.wa_count], self.sems.at[1, self.index, 1 + self.wa_count],
-                      {"pln": across(self.pln, 2)})
-
-    def begin(self):
-        for row in (0, 1):
-            self.core_copy(row).start()
-
-    def after_core(self):
-        for row in (0, 1):
-            self.core_copy(row).wait_recv()
-            mine = self.parts[row * 2 + self.core].astype(jnp.float32)
-            total = mine + self.got_core[self.index, row].astype(jnp.float32)
-            self.by_core[self.index, row] = total.astype(jnp.bfloat16)
-        for offset in range(1, self.wa_count):
-            self.wa_copy(offset).start()
-
-    def after_wa(self):
-        for offset in range(1, self.wa_count):
-            self.wa_copy(offset).wait_recv()
-        for row in (0, 1):
-            total = self.by_core[self.index, row, self.rows_of(self.wa), :].astype(jnp.float32)
-            for offset in range(1, self.wa_count):
-                total = total + self.got_wa[offset - 1, self.index, row].astype(jnp.float32)
-            self.by_wa[self.index, row] = total.astype(jnp.bfloat16)
-        self.row_copy().start()
-
-    def after_row(self):
-        self.row_copy().wait_recv()
-        total = self.by_wa[self.index, self.row].astype(jnp.float32) + self.got_row[self.index].astype(jnp.float32)
-        self.by_row[self.index] = total.astype(jnp.bfloat16)
-
-    def finish(self):
-        for row in (0, 1):
-            self.core_copy(row).wait_send()
-        for offset in range(1, self.wa_count):
-            self.wa_copy(offset).wait_send()
-        self.row_copy().wait_send()
+    )(dq, dkv, own, back, normed, inverse, hidden, mixed_one, mixed_two, branch_two, encoder, query_mat, out_mat, vecs, vg,
+      wide)
 
 
 def greet_all(grp_count, wa_count):
@@ -1036,14 +1087,16 @@
     pl.semaphore_wait(barrier, len(peers))
 
 
-def closing_kernel(grp_count, wa_count, reach, count, dq_ref, dkv_ref, own_ref, query_ref, content_ref, early_ref, vg_ref,
+def closing_kernel(grp_count, wa_count, reach, count, dq_ref, dkv_ref, own_ref, query_ref, content_ref, early_ref, wide_ref, vg_ref,
                    dq_out, kv_out, out_ref, vg_out,
                    dqsend, dqget, kvsend, kvget, total, mine, foldsend, foldget, parts, got_core, got_wa, got_row,
                    by_core, by_wa, by_row, got_grp, final, vsum, vgot, vall,
-                   fold_sems, load_sems, swap_sems, part_sems, red_sems, vec_sems, grp_sems, share_sems):
+                   fold_sems, load_sems, swap_sems, part_sems, wide_sem, red_sems, vec_sems, grp_sems, share_sems):
     grp, pln, wa = lax.axis_index("grp"), lax.axis_index("pln"), lax.axis_index("wa")
     tok = query_ref.shape[0]
     early = early_ref.shape[0]
+    wide = wide_ref.shape[0]
+    sets = ((0, wide), (wide, early + 1), (wide + early + 1, count - early - 1))
     size = 512 // wa_count
     slab = size // grp_count
     for p in range(PLANE):
@@ -1056,9 +1109,11 @@
     loads = [pltpu.make_async_copy(early_ref.at[i], parts.at[i], part_sems.at[i]) for i in range(early)]
     for l in loads:
         l.start()
+    wide_load = pltpu.make_async_copy(wide_ref, by_row.at[pl.ds(0, wide)], wide_sem)
+    wide_load.start()
     got, kept = (got_core, got_wa, got_row), (by_core, by_wa, by_row)
-    reds = [Reduce(i, early_ref.at[i] if i < early else parts.at[i], parts.at[i], got, kept, red_sems, wa_count)
-            for i in range(count)]
+    reds = [Reduce(i, early_ref.at[i] if i < early else parts.at[i], parts.at[i], got, kept, red_sems, wa_count,
+                   wide + i) for i in range(count)]
     for r in reds[:early]:
         r.begin()
     total[...] = own_ref[...]
@@ -1076,6 +1131,19 @@
         r.after_core()
     for stage in range(reach - 1, 0, -1):
         fold.grow(stage)
+    wide_load.wait()
+
+    def grp_copy(set_at, offset):
+        start, length = sets[set_at]
+        peer = lax.rem(grp + offset, grp_count)
+        some = pl.ds(start, length)
+        rows = pl.ds(pl.multiple_of(peer * slab, 8), slab)
+        return remote(by_row.at[some, rows], got_grp.at[offset - 1, some], grp_sems.at[0, set_at, offset - 1],
+                      grp_sems.at[1, set_at, offset - 1], {"grp": peer})
+
+    offsets = range(1, grp_count)
+    for o in offsets:
+        grp_copy(0, o).start()
     for r in reds[: early + 1]:
         r.after_wa()
     fold.total(total, kvsend)
@@ -1083,6 +1151,8 @@
     swap_kv.begin()
     for r in reds[: early + 1]:
         r.after_row()
+    for o in offsets:
+        grp_copy(1, o).start()
     for offset in range(4):
         swap_kv.arrived(offset)
     keys, values = halves(kvget)
@@ -1097,17 +1167,6 @@
     kv_out[:, :512] = keys
     kv_out[:, 512:] = values
 
-    def grp_copy(set_at, offset):
-        start, length = ((0, early + 1), (early + 1, count - early - 1))[set_at]
-        peer = lax.rem(grp + offset, grp_count)
-        some = pl.ds(start, length)
-        rows = pl.ds(pl.multiple_of(peer * slab, 8), slab)
-        return remote(by_row.at[some, rows], got_grp.at[offset - 1, some], grp_sems.at[0, set_at, offset - 1],
-                      grp_sems.at[1, set_at, offset - 1], {"grp": peer})
-
-    offsets = range(1, grp_count)
-    for o in offsets:
-        grp_copy(0, o).start()
     for r in reds[early + 1 :]:
         r.after_core()
     vec_core.wait_recv()
@@ -1133,7 +1192,7 @@
     own_rows = pl.ds(pl.multiple_of(grp * slab, 8), slab)
 
     def settle(set_at):
-        start, length = ((0, early + 1), (early + 1, count - early - 1))[set_at]
+        start, length = sets[set_at]
         some = pl.ds(start, length)
         for o in offsets:
             grp_copy(set_at, o).wait_recv()
@@ -1146,18 +1205,18 @@
         return out_ref.at[column, some, pl.ds(pl.multiple_of(source * slab, 8), slab)]
 
     def spread(set_at, offset):
-        start, length = ((0, early + 1), (early + 1, count - early - 1))[set_at]
+        start, length = sets[set_at]
         some = pl.ds(start, length)
         return remote(final.at[some], spot(pln, grp, some), share_sems.at[0, set_at, 0, offset],
                       share_sems.at[1, set_at, 0, offset], {"grp": lax.rem(grp + offset, grp_count)})
 
     def keep(set_at):
-        start, length = ((0, early + 1), (early + 1, count - early - 1))[set_at]
+        start, length = sets[set_at]
         some = pl.ds(start, length)
         return pltpu.make_async_copy(final.at[some], spot(pln, grp, some), share_sems.at[0, set_at, 0, 0])
 
     def give(set_at, kind, offset):
-        start, length = ((0, early + 1), (early + 1, count - early - 1))[set_at]
+        start, length = sets[set_at]
         some = pl.ds(start, length)
         source = lax.rem(grp + grp_count - offset, grp_count)
         column = pln if kind < 3 else across(pln, 2)
@@ -1165,14 +1224,18 @@
         return remote(there, there, share_sems.at[0, set_at, kind, offset], share_sems.at[1, set_at, kind, offset],
                       {"pln": across(pln, 2 if kind == 1 else 1)})
 
-    settle(0)
-    keep(0).start()
-    for o in offsets:
-        spread(0, o).start()
+    def share(set_at):
+        settle(set_at)
+        keep(set_at).start()
+        for o in offsets:
+            spread(set_at, o).start()
+
+    share(0)
+    share(1)
     for r in reds[early + 1 :]:
         r.after_row()
     for o in offsets:
-        grp_copy(1, o).start()
+        grp_copy(2, o).start()
     vec_row.wait_recv()
     vsum[3] = vsum[2] + vgot[wa_count]
     vec_grp = [remote(vsum.at[3], vall.at[wa_count + o], vec_sems.at[0, wa_count + o], vec_sems.at[1, wa_count + o],
@@ -1189,17 +1252,20 @@
         give(set_at, 1, offset).start()
         give(set_at, 2, offset).start()
 
+    def cross_over(set_at):
+        for o in everyone:
+            give(set_at, 1, o).wait_recv()
+            give(set_at, 3, o).start()
+
     for o in everyone:
         hand_out(0, o)
-    settle(1)
-    keep(1).start()
-    for o in offsets:
-        spread(1, o).start()
-    for o in everyone:
-        give(0, 1, o).wait_recv()
-        give(0, 3, o).start()
     for o in everyone:
         hand_out(1, o)
+    share(2)
+    cross_over(0)
+    cross_over(1)
+    for o in everyone:
+        hand_out(2, o)
     for v in vec_grp:
         v.wait_recv()
     ordered = jnp.zeros_like(vsum[3])
@@ -1209,14 +1275,12 @@
             piece = piece + jnp.where(lax.rem(grp + grp_count - o, grp_count) == g, vall[wa_count + o], 0.0)
         ordered = ordered + piece
     vg_out[...] = ordered
-    for o in everyone:
-        give(1, 1, o).wait_recv()
-        give(1, 3, o).start()
-    for set_at in (0, 1):
+    cross_over(2)
+    for set_at in range(3):
         for o in everyone:
             give(set_at, 2, o).wait_recv()
             give(set_at, 3, o).wait_recv()
-    for set_at in (0, 1):
+    for set_at in range(3):
         for o in everyone:
             for kind in (1, 2, 3):
                 give(set_at, kind, o).wait_send()
@@ -1232,9 +1296,10 @@
     swap_kv.finish()
 
 
-def run_closing(grp_count, wa_count, dq, dkv, own, query, content, early, vg):
+def run_closing(grp_count, wa_count, dq, dkv, own, query, content, early, wide, vg):
     tok = query.shape[0]
     count = early.shape[0] + 3
+    every = count + wide.shape[0]
     reach = min(grp_count - 1, (DOCLEN + PLANE * tok - 2) // (PLANE * tok))
     size = 512 // wa_count
     slab = size // grp_count
@@ -1244,27 +1309,27 @@
     steps = wa_count + 2
     return pl.pallas_call(
         functools.partial(closing_kernel, grp_count, wa_count, reach, count),
-        out_shape=(shape((tok, 512), low), shape((tok, 1024), low), shape((PLANE, count, size, 128), low),
+        out_shape=(shape((tok, 512), low), shape((tok, 1024), low), shape((PLANE, every, size, 128), low),
                    shape(vg.shape, full)),
-        in_specs=[VMEM, ANY, VMEM, VMEM, VMEM, ANY, VMEM],
+        in_specs=[VMEM, ANY, VMEM, VMEM, VMEM, ANY, ANY, VMEM],
         out_specs=(VMEM, VMEM, ANY, VMEM),
         scratch_shapes=[pairs] * 2 + fold_scratch(tok, reach) + [
             pltpu.VMEM((count, PLANE, 512, 128), low), pltpu.VMEM((count, 2, 512, 128), low),
             pltpu.VMEM((max(1, wa_count - 1), count, 2, size, 128), low), pltpu.VMEM((count, size, 128), low),
-            pltpu.VMEM((count, 2, 512, 128), low), pltpu.VMEM((count, 2, size, 128), low), pltpu.VMEM((count, size, 128), low),
-            pltpu.VMEM((grp_count - 1, count, slab, 128), low), pltpu.VMEM((count, slab, 128), low),
+            pltpu.VMEM((count, 2, 512, 128), low), pltpu.VMEM((count, 2, size, 128), low), pltpu.VMEM((every, size, 128), low),
+            pltpu.VMEM((grp_count - 1, every, slab, 128), low), pltpu.VMEM((every, slab, 128), low),
             pltpu.VMEM((4,) + vg.shape, full), pltpu.VMEM((wa_count + 1,) + vg.shape, full),
             pltpu.VMEM((wa_count + grp_count,) + vg.shape, full),
-            DMA((2, 2, reach, PLANE)), DMA((2, max(1, reach - 1))), DMA((2, 2, 4)), DMA((early.shape[0],)),
-            DMA((2, count, steps)), DMA((2, wa_count + grp_count)), DMA((2, 2, grp_count - 1)), DMA((2, 2, 4, grp_count))],
+            DMA((2, 2, reach, PLANE)), DMA((2, max(1, reach - 1))), DMA((2, 2, 4)), DMA((early.shape[0],)), DMA,
+            DMA((2, count, steps)), DMA((2, wa_count + grp_count)), DMA((2, 3, grp_count - 1)), DMA((2, 3, 4, grp_count))],
         cost_estimate=pl.CostEstimate(flops=75000000000, bytes_accessed=0, transcendentals=0),
         compiler_params=pltpu.CompilerParams(collective_id=9, has_side_effects=True, vmem_limit_bytes=60 << 20),
-    )(dq, dkv, own, query, content, early, vg)
+    )(dq, dkv, own, query, content, early, wide, vg)
 
 
 def centre_kernel(wa_count, vec_at, attended_ref, hidden_ref, cotangent_ref, out_mat_ref, expand_ref, shrink_ref, vec_ref,
-                  layer_out, mixed_out, back_out, branch_out, do_out, grad_shrink, grad_expand, vg_out,
-                  sendbuf, getbuf, dosend, doget, slopes, actives, swap_sems):
+                  layer_out, mixed_out, back_out, branch_out, do_out, grads_out, vg_out,
+                  sendbuf, getbuf, dosend, doget, slopes, actives, grads, swap_sems, out_sems):
     tok = hidden_ref.shape[0]
     for p in range(PLANE):
         sendbuf[p] = attended_ref[p * tok : p * tok + tok, :].astype(jnp.bfloat16)
@@ -1320,14 +1385,26 @@
     vg_out[7:8, :] = gain_grad.reshape(1, 512)
     vg_out[8:9, :] = shift_grad.reshape(1, 512)
     vg_out[9:10, :] = column_sum(branch).reshape(1, 512)
+    size = 512 // wa_count
+    saves = [pltpu.make_async_copy(grads.at[i], grads_out.at[i], out_sems.at[i]) for i in range(2 * chunks)]
     for c in range(chunks):
         span = slice(c * width, c * width + width)
-        grad_shrink[span, :] = dot(actives[:, span], grad, 0, 0).astype(jnp.bfloat16)
-        grad_expand[:, span] = dot(low, steps[c], 0, 0).astype(jnp.bfloat16)
+        store_blocks(grads.at[c], dot(low, steps[c], 0, 0))
+        saves[c].start()
+        value = dot(actives[:, span], grad, 0, 0).astype(jnp.bfloat16)
+        for piece in range(width // size):
+            owner, index = divmod(c * (width // size) + piece, chunks)
+            for column in range(PLANE):
+                grads[chunks + index, column, owner * size : owner * size + size, :] = value[
+                    piece * size : piece * size + size, column * 128 : column * 128 + 128]
+    for c in range(chunks):
+        saves[chunks + c].start()
     for offset in range(4):
         swap_do.arrived(offset)
     for p in range(PLANE):
         do_out[p * tok : p * tok + tok, :] = doget[p]
+    for save in saves:
+        save.wait()
     swap.finish()
     swap_do.finish()
 
@@ -1341,24 +1418,29 @@
     return pl.pallas_call(
         functools.partial(centre_kernel, wa_count, vec_at),
         out_shape=(shape((tok, 512), full), shape((tok, 512), low), shape((tok, 512), full), shape((tok, 512), low),
-                   shape((PLANE * tok, 128), low), shape(shrink.shape, low), shape(expand.shape, low), shape((24, 512), full)),
+                   shape((PLANE * tok, 128), low), shape((2 * wide // 512, PLANE, 512, 128), low), shape((24, 512), full)),
         in_specs=[VMEM] * 7,
-        out_specs=(VMEM,) * 8,
-        scratch_shapes=[pairs] * 4 + [pltpu.VMEM((tok, wide), full), pltpu.VMEM((tok, wide), low), DMA((2, 2, 4))],
+        out_specs=(VMEM,) * 5 + (ANY, VMEM),
+        scratch_shapes=[pairs] * 4 + [pltpu.VMEM((tok, wide), full), pltpu.VMEM((tok, wide), low),
+            pltpu.VMEM((2 * wide // 512, PLANE, 512, 128), low), DMA((2, 2, 4)), DMA((2 * wide // 512,))],
         compiler_params=pltpu.CompilerParams(collective_id=3, has_side_effects=True, vmem_limit_bytes=60 << 20),
     )(attended, hidden, cotangent, out_mat, expand, shrink, vecs)
 
 
 def last_kernel(wa_count, shares, at_ref, late_ref, sums_ref, dq_ref, dkv_ref, back_ref, query_mat, key_mat, value_mat,
-                expand_ref, shrink_ref, query_out, content_out, expand_out, shrink_out, *outs):
-    count = late_ref.shape[1]
-    for i in range(count):
-        for c in range(PLANE):
-            outs[i][:, c * 128 : c * 128 + 128] = late_ref[c, i].astype(jnp.float32)
+                query_out, content_out, expand_out, shrink_out, *outs):
+    wide = expand_out.shape[1] // 512
+    size = late_ref.shape[2]
+    count = late_ref.shape[1] - 2 * wide
+    for c in range(PLANE):
+        span = slice(c * 128, c * 128 + 128)
+        for i in range(count):
+            outs[i][:, span] = late_ref[c, 2 * wide + i].astype(jnp.float32)
+        for i in range(wide):
+            expand_out[:, i * 512 + c * 128 : i * 512 + c * 128 + 128] = late_ref[c, i].astype(jnp.float32)
+            shrink_out[i * size : i * size + size, span] = late_ref[c, wide + i].astype(jnp.float32)
     query_out[...] = back_ref[...] + dot(dq_ref[...], query_mat[...], 1, 1)
     content_out[...] = dot(dkv_ref[:, :512], key_mat[...], 1, 1) + dot(dkv_ref[:, 512:], value_mat[...], 1, 1)
-    expand_out[...] = expand_ref[...].astype(jnp.float32)
-    shrink_out[...] = shrink_ref[...].astype(jnp.float32)
     at = 0
     for i, share in enumerate(shares):
         used = share * wa_count // 512
@@ -1370,27 +1452,20 @@
         outs[count + i][...] = mine.reshape(share)
 
 
-def run_last(wa_count, shares, at, late, sums, dq, dkv, back, query_mat, key_mat, value_mat, expand, shrink):
+def run_last(wa_count, wide, shares, at, late, sums, dq, dkv, back, query_mat, key_mat, value_mat):
     full = jnp.float32
     shape = jax.ShapeDtypeStruct
     tok = dq.shape[0]
-    out_shape = [shape((tok, 512), full), shape((tok, 512), full), shape(expand.shape, full), shape(shrink.shape, full)]
-    out_shape += [shape((late.shape[2], 512), full)] * late.shape[1] + [shape((s,), full) for s in shares]
+    out_shape = [shape((tok, 512), full), shape((tok, 512), full), shape((late.shape[2], wide), full),
+                 shape((wide // wa_count, 512), full)]
+    out_shape += [shape((late.shape[2], 512), full)] * (late.shape[1] - wide // 256) + [shape((s,), full) for s in shares]
     return pl.pallas_call(
         functools.partial(last_kernel, wa_count, shares),
         out_shape=tuple(out_shape),
-        in_specs=[SMEM] + [VMEM] * 10,
+        in_specs=[SMEM] + [VMEM] * 8,
         out_specs=tuple([VMEM] * len(out_shape)),
         compiler_params=pltpu.CompilerParams(vmem_limit_bytes=60 << 20),
-    )(at, late, sums, dq, dkv, back, query_mat, key_mat, value_mat, expand, shrink)
-
-
-def scatter_wide(grad):
-    return lax.psum_scatter(grad.astype(jnp.bfloat16), "wa", scatter_dimension=0, tiled=True)
-
-
-def sum_wide(share):
-    return lax.psum(share, ("grp", "pln"))
+    )(at, late, sums, dq, dkv, back, query_mat, key_mat, value_mat)
 
 
 def shards(
@@ -1454,30 +1529,25 @@
         grp_count, wa_count, attended_one, source, self_out_mat, cross_query_mat, vec_all, vec_at, kv_two_own,
         expand_weight, shrink_weight)
     attended_two, total_two = attend_forward(False, lens, own, pair_two, cross_marks, kv_two, cross_keys)
-    layer_out, mixed_two, back_two, branch_two, do_two, grad_shrink_mat, grad_expand_mat, lines = run_centre(
+    layer_out, mixed_two, back_two, branch_two, do_two, wide, lines = run_centre(
         wa_count, vec_at, attended_two, hidden_one, out_grad[0], cross_out_mat, expand_mat, shrink_mat, vec_all)
-    grad_shrink_mat = scatter_wide(grad_shrink_mat)
-    grad_expand_mat = scatter_wide(grad_expand_mat)
     dq_two, dkv_two, own_two = attend_backward(False, lens, own, pair_two, cross_marks, kv_two, cross_keys,
         attended_two, total_two, do_two)
-    do_one, back_one, kv_two_grad, early, lines = run_turn(grp_count, wa_count, vec_at, dq_two, dkv_two, own_two, back_two,
+    do_one, back_one, kv_two_grad, early, lines, wide = run_turn(grp_count, wa_count, vec_at, dq_two, dkv_two, own_two, back_two,
         normed_one, inverse_one, hidden_one, mixed_one, mixed_two, branch_two, encoder_output, cross_query_mat, self_out_mat,
-        vec_all, lines)
-    do_one, grad_shrink_mat, grad_expand_mat = lax.optimization_barrier((do_one, grad_shrink_mat, grad_expand_mat))
-    grad_shrink_mat = sum_wide(grad_shrink_mat)
-    grad_expand_mat = sum_wide(grad_expand_mat)
+        vec_all, lines, wide)
     key_two_low, value_two_low = kv_two_grad[:, :512], kv_two_grad[:, 512:]
     encoder_grad = right_product(key_two_low, cross_key_matrix) + right_product(value_two_low, cross_value_mat)
     dq_one, dkv_one, own_one = attend_backward(True, lens, own, pair_one, self_marks, kv_one, self_keys,
         attended_one, total_one, do_one)
     query_one_low, kv_one_grad, late, sums = run_closing(grp_count, wa_count, dq_one, dkv_one, own_one, source,
-        content_states, early, lines)
+        content_states, early, wide, lines)
     shares = tuple(v.shape[0] for v in (norm_three_gain, norm_three_shift, shrink_bias, expand_bias, norm_two_gain,
         norm_two_shift, cross_out_bias, norm_one_gain, norm_one_shift, self_out_bias, cross_query_bias, cross_value_bias,
         self_query_bias, self_value_bias))
-    query_grad, content_grad, expand_grad, shrink_grad, *rest = run_last(wa_count, shares,
+    query_grad, content_grad, expand_grad, shrink_grad, *rest = run_last(wa_count, expand_weight.shape[1], shares,
         lax.axis_index("wa")[None].astype(jnp.int32), late, sums, query_one_low, kv_one_grad, back_one, self_query_mat,
-        self_key_matrix, self_value_mat, grad_expand_mat, grad_shrink_mat)
+        self_key_matrix, self_value_mat)
     names = ("cross_out", "cross_query", "self_out", "cross_key", "cross_value", "self_query", "self_key", "self_value")
     mat = dict(zip(names, rest))
     names = ("gain_three", "shift_three", "shrink", "expand", "gain_two", "shift_two", "cross_out", "gain_one", "shift_one",

time: 357 us -> 316 us (0.89)
  waiting for transfers between devices: 14.9 us -> 0 us
  Pallas kernels: 319 us -> 305 us
  between operations: 13.9 us -> 0.78 us
    pallas_call x2, Pallas kernels: 57.3 us -> 36 us  [attend_backward(): pl.pallas_call(functools.partial(backward_kernel, ranked), out_shape=(jax...]
    psum x1 -> x0, waiting for transfers between devices: 14.2 us -> none  [sum_wide(): return lax.psum(share, ('grp', 'pln'))]
    pallas_call x1, Pallas kernels: 33.2 us -> 46.9 us  [run_turn(): pl.pallas_call(functools.partial(turn_kernel, grp_count, wa_count, reach,...]
    pallas_call x2, Pallas kernels: 27.2 us -> 19.4 us  [attend_forward(): pl.pallas_call(functools.partial(forward_kernel, ranked), out_shape=(jax....]
  transfers between devices with their start and end apart: 3 -> 0, of which waited for: 1 -> 0; matrix products, arithmetic and copies ran while one was open for 1% -> 0% of each run, Pallas kernels for 45% -> 0%
where the time goes in v1:
time: 316 us; the launch traced here: 310 us
  Pallas kernels  305 us (97%)
  matrix products  3.36 us (1%)
    pallas_call x1, Pallas kernels, run_closing(): pl.pallas_call(functools.partial(closing_kernel, grp_count, wa_count, rea...  98.2 us
    pallas_call x1, Pallas kernels, run_turn(): pl.pallas_call(functools.partial(turn_kernel, grp_count, wa_count, reach,...  46.9 us
    pallas_call x1, Pallas kernels, run_opening(): pl.pallas_call(functools.partial(opening_kernel, grp_count, wa_count, rea...  45.5 us
    pallas_call x2, Pallas kernels, attend_backward(): pl.pallas_call(functools.partial(backward_kernel, ranked), out_shape=(jax...  36 us
    pallas_call x1, Pallas kernels, run_middle(): pl.pallas_call(functools.partial(middle_kernel, grp_count, wa_count, reac...  32.3 us
    pallas_call x2, Pallas kernels, attend_forward(): pl.pallas_call(functools.partial(forward_kernel, ranked), out_shape=(jax....  19.4 us
    pallas_call x1, Pallas kernels, run_centre(): pl.pallas_call(functools.partial(centre_kernel, wa_count, vec_at), out_sh...  19.2 us
    pallas_call x1, Pallas kernels, run_last(): pl.pallas_call(functools.partial(last_kernel, wa_count, shares), out_shap...  7.48 us

profile of v1, /device:TPU:0, one launch (start us, length us, event | category | flops | bytes accessed | tf_op | source)
XLA Modules:
  0.0 309.9 jit_solution(9467619938245896473)
XLA Ops:
  0.7 45.5 %shard_map.510 = (bf16[512,512]{1,0:T(8,128)(2,1)}, bf16[512,512]{1,0:T(8,128)(2,1)}, bf16[512,512]{1,0:T(8,128)(2,1)}, bf16[512,512]{1,0:T(8,128)(2,1)}, bf16[5...) custom-call(s32[1,4]{1,0:T(1,128)} %lens_ref.9, ...), custom_call_target="tpu_custom_call" | custom-call | flops 38000001024 | tf_op jit(solution)/shard_map/pallas_call | solution.py:660
  46.2 9.7 %shard_map.511 = (f32[1024,128]{1,0:T(8,128)}, f32[1024,128]{1,0:T(8,128)}) custom-call(s32[1,4]{1,0:T(1,128)} %lens_ref.9, s32[1]{0:T(128)} %bitcast.own_ref, bf16[1024,128]{1,0:T(8,128)(2,1)} %get-tuple-element.105.q_ref, bf16[1024,128]{1,0:T(8,128)(2,1)} %get-tuple-element.106.qm_ref, bf16[4096,256]{1,0:T(8,128)(2,1)} %get-tuple-element.107.kv_ref, ...), custom_call_target="tpu_custom_call" | custom-call | flops 12000000000 | tf_op jit(solution)/shard_map/pallas_call | solution.py:128
  55.9 32.3 %shard_map.512 = (f32[256,512]{1,0:T(8,128)}, f32[256,512]{1,0:T(8,128)}, f32[256,128]{1,0:T(8,128)}, bf16[256,512]{1,0:T(8,128)(2,1)}, bf16[1024,128]{1,0:T(8,1...) custom-call(f32[1024,128]{1,0:T(8,128)} %get-tuple-element.109.attended_ref.o_ref, ...), custom_call_target="tpu_custom_call" | custom-call | flops 30000001024 | tf_op jit(solution)/shard_map/pallas_call | solution.py:744
  88.2 9.6 %shard_map.513 = (f32[1024,128]{1,0:T(8,128)}, f32[1024,128]{1,0:T(8,128)}) custom-call(s32[1,4]{1,0:T(1,128)} %lens_ref.9, s32[1]{0:T(128)} %bitcast.own_ref, bf16[1024,128]{1,0:T(8,128)(2,1)} %get-tuple-element.114.q_ref, bf16[1024,128]{1,0:T(8,128)(2,1)} %get-tuple-element.115.qm_ref, bf16[4096,256]{1,0:T(8,128)(2,1)} %get-tuple-element.116.kv_ref, ...), custom_call_target="tpu_custom_call" | custom-call | flops 12000000000 | tf_op jit(solution)/shard_map/pallas_call | solution.py:128
  97.9 19.2 %shard_map.514 = (f32[256,512]{1,0:T(8,128)}, bf16[256,512]{1,0:T(8,128)(2,1)}, f32[256,512]{1,0:T(8,128)}, bf16[256,512]{1,0:T(8,128)(2,1)}, bf16[1024,128]{1,0...) custom-call(f32[1024,128]{1,0:T(8,128)} %get-tuple-element.118.attended_ref.o_ref, ...), custom_call_target="tpu_custom_call" | custom-call | tf_op jit(solution)/shard_map/pallas_call | solution.py:1418
  117.0 18.0 %shard_map.515 = (bf16[1024,128]{1,0:T(8,128)(2,1)}, bf16[4096,256]{1,0:T(8,128)(2,1)}, f32[1024,256]{1,0:T(8,128)}) custom-call(s32[1,4]{1,0:T(1,128)} %lens_ref.9, s32[1]{0:T(128)} %bitcast.own_ref, bf16[1024,128]{1,0:T(8,128)(2,1)} %get-tuple-element.114.q_ref, bf16[1024,128]{1,0:T(8,128)(2,1)} %get-tuple-element.115.qm_ref, ...), custom_call_target="tpu_custom_call" | custom-call | flops 25999998976 | tf_op jit(solution)/shard_map/pallas_call | solution.py:235
  135.0 0.0 copy-start.2
  135.0 0.0 copy-start
  135.0 46.9 %shard_map.516 = (bf16[1024,128]{1,0:T(8,128)(2,1)}, f32[256,512]{1,0:T(8,128)}, bf16[256,1024]{1,0:T(8,128)(2,1)}, bf16[5,4,512,128]{3,2,1,0:T(8,128)(2,1)}, f3...) custom-call(bf16[1024,128]{1,0:T(8,128)(2,1)} %get-tuple-element.127.dq_ref, bf16[4096,256]{1,0:T(8,128)(2,1)} %get-tuple-element.128.dkv_ref, ...), custom_call_target="tpu_custom_call" | custom-call | flops 32000000000 | tf_op jit(solution)/shard_map/pallas_call | solution.py:1061
  181.9 0.0 copy-done.2
  181.9 1.3 fusion.2
  183.2 0.0 copy-done
  183.2 2.1 fusion
  185.3 18.0 %shard_map.517 = (bf16[1024,128]{1,0:T(8,128)(2,1)}, bf16[4096,256]{1,0:T(8,128)(2,1)}, f32[1024,256]{1,0:T(8,128)}) custom-call(s32[1,4]{1,0:T(1,128)} %lens_ref.9, s32[1]{0:T(128)} %bitcast.own_ref, bf16[1024,128]{1,0:T(8,128)(2,1)} %get-tuple-element.105.q_ref, bf16[1024,128]{1,0:T(8,128)(2,1)} %get-tuple-element.106.qm_ref, ...), custom_call_target="tpu_custom_call" | custom-call | flops 25999998976 | tf_op jit(solution)/shard_map/pallas_call | solution.py:235
  203.3 98.2 %shard_map.518 = (bf16[256,512]{1,0:T(8,128)(2,1)}, bf16[256,1024]{1,0:T(8,128)(2,1)}, bf16[4,16,256,128]{3,2,1,0:T(8,128)(2,1)}, f32[24,512]{1,0:T(8,128)}) custom-call(bf16[1024,128]{1,0:T(8,128)(2,1)} %get-tuple-element.139.dq_ref, bf16[4096,256]{1,0:T(8,128)(2,1)} %get-tuple-element.140.dkv_ref, f32[1024,256]{1,0:T(8,128)} %get-tuple-element.141.own_ref, ...), custom_call_target="tpu_custom_call" | custom-call | flops 74999996416 | tf_op jit(solution)/shard_map/pallas_call | solution.py:1310
  301.6 0.0 copy-start.1
  301.6 7.5 %shard_map.519 = (f32[256,512]{1,0:T(8,128)}, f32[256,512]{1,0:T(8,128)}, f32[256,2048]{1,0:T(8,128)}, f32[1024,512]{1,0:T(8,128)}, f32[256,512]{1,0:T(8,128)}, ...) custom-call(s32[1]{0:T(128)} %bitcast.6.at_ref, ...), custom_call_target="tpu_custom_call" | custom-call | tf_op jit(solution)/shard_map/pallas_call | solution.py:1462
  309.1 0.0 copy-done.1
  309.1 0.8 copy.60
Async XLA Ops:
  135.0 46.9 %copy-start.2 = (bf16[512,512]{1,0:T(8,128)(2,1)S(1)}, bf16[512,512]{1,0:T(8,128)(2,1)}, u32[]{:S(2)}) copy-start(bf16[512,512]{1,0:T(8,128)(2,1)} %get-tuple-element.156) | copy-start | bytes 1572868
  135.0 48.2 %copy-start = (bf16[512,512]{1,0:T(8,128)(2,1)S(1)}, bf16[512,512]{1,0:T(8,128)(2,1)}, u32[]{:S(2)}) copy-start(bf16[512,512]{1,0:T(8,128)(2,1)} %get-tuple-element.157) | copy-start | bytes 1572868
  301.6 7.5 %copy-start.1 = (f32[256,512]{1,0:T(8,128)S(1)}, f32[256,512]{1,0:T(8,128)}, u32[]{:S(2)}) copy-start(f32[256,512]{1,0:T(8,128)} %get-tuple-element.123) | copy-start | bytes 1572868
